TPU v7x, 512 devices: a whole 4x8x8 slice. The times are simulated.
512 devices in a mesh: ctx: 128 (over x_hi, y, z), tensor: 4 (over x_lo, core).
Axes of the slice: x: 4 (x_hi: 2, x_lo: 2; x = x_hi * 2 + x_lo), y: 8, z: 8, core: 2. Of those that a mesh axis runs over, the one named last changes fastest.
Arguments:
- queries: bfloat16 [65536, 4096], P(('ctx', 'tensor')), may hold values from -6 to 6
- keys: bfloat16 [65536, 1024], P(('ctx', 'tensor')), may hold values from -10 to 10
- values: bfloat16 [65536, 1024], P(('ctx', 'tensor')), may hold values from -6 to 6
- mid_offsets: int32 [8], P('tensor'), may hold values from 0 to 7
- far_offsets: int32 [8], P('tensor'), may hold values from 0 to 63
Outputs:
- attended: bfloat16 [65536, 4096], P(('ctx', 'tensor'))
All inputs are finite; a program needn't handle non-finite values.
Results may differ from a plain program's by a relative error of at most 0.003.
Values may be sent and summed in bfloat16 or wider, within the bound.
A program may use at most 64 MiB of HBM per device.

v0:
```python
import jax
import jax.numpy as jnp
from jax import lax
from jax.sharding import PartitionSpec as P

HEADS = 32
KV_HEADS = 8
HEAD_DIM = 128
RATE_MID = 8
RATE_FAR = 64


NEG_FILL = -1e30


def passed_along(value, axis, steps):
    count = lax.axis_size(axis)
    leading, last = (max(0, -steps), min(count, count - steps))
    return lax.ppermute(value, axis, [(source, source + steps) for source in range(leading, last)])


def partner_2(value, axis, stride):
    mask = 2**stride
    pairs = [(source, source ^ mask) for source in range(lax.axis_size(axis))]
    return lax.ppermute(value, axis, pairs)


def head_stats(query_rows, key_rows, value_rows, allowed, scale_factor):
    scores = (
        jnp.einsum("agd,bd->agb", query_rows, key_rows, preferred_element_type=jnp.float32)
        * scale_factor
    )
    scores = jnp.where(allowed[:, None, :], scores, NEG_FILL)
    maxima = jnp.max(scores, axis=-1)
    powers = jnp.exp(scores - maxima[..., None])
    totals = jnp.sum(powers, axis=-1)
    weights = powers.astype(jnp.bfloat16)
    weighted = jnp.einsum("agb,bd->agd", weights, value_rows, preferred_element_type=jnp.float32)
    return (maxima, totals, weighted)


def branch_stats(query_rows, kv_rows, allowed, scale_factor):
    query_heads = query_rows.transpose(1, 0, 2, 3)
    key_heads = kv_rows[:, 0].transpose(1, 0, 2)
    value_heads = kv_rows[:, 1].transpose(1, 0, 2)

    def one_head(items):
        return head_stats(items[0], items[1], items[2], allowed, scale_factor)

    return lax.map(one_head, (query_heads, key_heads, value_heads))


def pick_rows(rows, offsets, rate, kv_dim):
    shaped = rows.reshape((rows.shape[0] // rate, rate) + rows.shape[1:])
    chosen = jnp.arange(rate, dtype=jnp.int32)[:, None] == offsets[None, :]
    hit_shape = [1] * shaped.ndim
    hit_shape[1] = rate
    hit_shape[kv_dim + 1] = offsets.shape[0]
    kept = jnp.where(chosen.reshape(hit_shape), shaped, jnp.zeros((), rows.dtype))
    return jnp.sum(kept, axis=1)


def spread_stats(stats, offsets, rate):
    maxima, totals, weighted = stats
    kv_local = maxima.shape[0]
    per_group = maxima.shape[2]
    chosen = jnp.arange(rate, dtype=jnp.int32)[None, :] == offsets[:, None]
    maxima = jnp.where(chosen[:, None, :, None], maxima[:, :, None, :], NEG_FILL).reshape(
        kv_local, -1, per_group
    )
    totals = jnp.where(chosen[:, None, :, None], totals[:, :, None, :], jnp.float32(0.0)).reshape(
        kv_local, -1, per_group
    )
    weighted = jnp.where(chosen[:, None, :, None, None], weighted[:, :, None], jnp.float32(0.0))
    return (maxima, totals, weighted.reshape(kv_local, -1, per_group, weighted.shape[-1]))


def join_halves(mine, partner, upper_half):
    return jnp.where(
        upper_half, jnp.concatenate([partner, mine], 0), jnp.concatenate([mine, partner], 0)
    )


def on_device(queries, keys, values, mid_offsets, far_offsets):
    queries, keys, values = (
        lax.all_to_all(queries, "tensor", split_axis=1, concat_axis=0, tiled=True),
        lax.all_to_all(keys, "tensor", split_axis=1, concat_axis=0, tiled=True),
        lax.all_to_all(values, "tensor", split_axis=1, concat_axis=0, tiled=True),
    )
    tok_rows = queries.shape[0]
    kv_local = mid_offsets.shape[0]
    per_group = HEADS // KV_HEADS
    scale_factor = HEAD_DIM ** (-0.5)
    query_rows = queries.reshape(tok_rows, kv_local, per_group, HEAD_DIM)
    kv_rows = jnp.stack(
        [keys.reshape(tok_rows, kv_local, HEAD_DIM), values.reshape(tok_rows, kv_local, HEAD_DIM)],
        axis=1,
    )
    ctx_count = lax.axis_size("ctx")
    ctx_place = lax.axis_index("ctx")
    team_size = min(16, ctx_count)
    team_bits = team_size.bit_length() - 1
    previous = passed_along(kv_rows, "ctx", 1)
    near_keys = jnp.concatenate([previous, kv_rows], 0)
    query_index = jnp.arange(tok_rows)[:, None]
    key_index = jnp.arange(2 * tok_rows)[None, :]
    near_allowed = jnp.where(
        key_index >= tok_rows,
        key_index - tok_rows <= query_index,
        (key_index > query_index) & (ctx_place > 0),
    )
    near_stats = branch_stats(query_rows, near_keys, near_allowed, scale_factor)
    mid_queries = pick_rows(query_rows, mid_offsets, RATE_MID, 1)
    mid_kv = pick_rows(kv_rows, mid_offsets, RATE_MID, 2)
    far_queries = pick_rows(query_rows, far_offsets, RATE_FAR, 1)
    far_kv = pick_rows(kv_rows, far_offsets, RATE_FAR, 2)
    mid_count = tok_rows // RATE_MID
    far_count = tok_rows // RATE_FAR
    mid_all = mid_kv
    for bit_index in range(team_bits):
        upper_half = ctx_place // (1 << bit_index) % 2 == 1
        partner = partner_2(mid_all, "ctx", bit_index)
        mid_all = join_halves(mid_all, partner, upper_half)
    far_all = lax.all_gather(far_kv, "ctx", axis=0, tiled=True)
    mid_position = ctx_place % team_size * mid_count + jnp.arange(mid_count)[:, None]
    mid_allowed = jnp.arange(team_size * mid_count)[None, :] <= mid_position
    mid_stats = spread_stats(
        branch_stats(mid_queries, mid_all, mid_allowed, scale_factor), mid_offsets, RATE_MID
    )
    far_position = ctx_place * far_count + jnp.arange(far_count)[:, None]
    far_allowed = jnp.arange(ctx_count * far_count)[None, :] <= far_position
    far_stats = spread_stats(
        branch_stats(far_queries, far_all, far_allowed, scale_factor), far_offsets, RATE_FAR
    )
    highest = jnp.maximum(jnp.maximum(near_stats[0], mid_stats[0]), far_stats[0])
    denominator = jnp.zeros_like(highest)
    numerator = jnp.zeros(near_stats[2].shape, jnp.float32)
    for stats in (near_stats, mid_stats, far_stats):
        factor = jnp.exp(stats[0] - highest)
        denominator = denominator + factor * stats[1]
        numerator = numerator + factor[..., None] * stats[2]
    attended = (numerator / denominator[..., None]).astype(jnp.bfloat16)
    attended = attended.transpose(1, 0, 2, 3).reshape(tok_rows, kv_local * per_group * HEAD_DIM)
    return lax.all_to_all(attended, "tensor", split_axis=0, concat_axis=1, tiled=True)


def solution(mesh):
    in_specs = (
        P(("ctx", "tensor"), None),
        P(("ctx", "tensor"), None),
        P(("ctx", "tensor"), None),
        P("tensor"),
        P("tensor"),
    )
    out_specs = P(("ctx", "tensor"), None)
    return jax.shard_map(
        on_device, mesh=mesh, in_specs=in_specs, out_specs=out_specs, check_vma=False
    )
```

profile of v0, /device:TPU:1, one launch (start us, length us, event | category | flops | bytes accessed | tf_op | source)
XLA Modules:
  0.0 212.3 jit_solution(1212099369880963147)
XLA Ops:
  6.5 1.9 copy.30
  8.4 10.4 %all-to-all-start.1 = ((bf16[128,4,256]{0,2,1:T(8,128)(2,1)}), bf16[128,4,256]{0,2,1:T(8,128)(2,1)S(1)}, u32[]{:S(2)}, u32[]{:S(2)}) async-start(bf16[128,4,256]{0,2,1:T(8,128)(2,1)} %bitcast.3), calls=%async_computation.1 | async-start | bytes 524288 | tf_op jit(solution)/shard_map/all_to_all | solution.py:87
  19.5 0.7 iota_compare_fusion.8
  20.2 0.7 iota_compare_fusion.6
  20.9 0.7 broadcast_in_dim.314
  21.6 0.7 broadcast_in_dim.303
  22.3 1.8 copy.32
  24.1 1.3 copy.28
  25.5 3.5 %all-to-all-start.2 = ((bf16[128,4,256]{0,2,1:T(8,128)(2,1)}), bf16[128,4,256]{0,2,1:T(8,128)(2,1)S(1)}, u32[]{:S(2)}, u32[]{:S(2)}) async-start(bf16[128,4,256]{0,2,1:T(8,128)(2,1)} %bitcast.5), calls=%async_computation.2 | async-start | bytes 524288 | tf_op jit(solution)/shard_map/all_to_all | solution.py:88
  29.2 4.9 %all-to-all-done.2 = bf16[128,4,256]{0,2,1:T(8,128)(2,1)S(1)} async-done(((bf16[128,4,256]{0,2,1:T(8,128)(2,1)}), bf16[128,4,256]{0,2,1:T(8,128)(2,1)S(1)}, u32[]{:S(2)}, u32[]{:S(2)}) %all-to-all-start.2) | async-done | bytes 262176 | tf_op jit(solution)/shard_map/all_to_all | solution.py:88
  34.2 4.4 %all-to-all-start = ((bf16[128,4,1024]{0,2,1:T(8,128)(2,1)}), bf16[128,4,1024]{0,2,1:T(8,128)(2,1)S(1)}, u32[]{:S(2)}, u32[]{:S(2)}) async-start(bf16[128,4,1024]{0,2,1:T(8,128)(2,1)} %bitcast), calls=%async_computation | async-start | bytes 2097152 | tf_op jit(solution)/shard_map/all_to_all | solution.py:86
  39.2 1.9 collective-permute-start.1
  41.7 3.1 %collective-permute-done.1 = bf16[64,2,2,128]{3,2,1,0:T(2,128)(2,1)S(1)} collective-permute-done((bf16[64,2,2,128]{3,2,1,0:T(2,128)(2,1)S(1)}, bf16[64,2,2,128]{3,2,1,0:T(2,128)(2,1)S(1)}, u32[]{:S(2)}, u32[]{:S(2)}) %collective-permute-start.1) | collective-permute-done | bytes 65568 | tf_op jit(solution)/shard_map/ppermute | solution.py:25
  45.0 1.9 collective-permute-start.2
  47.6 2.5 %collective-permute-start = (bf16[512,2,2,128]{3,2,0,1:T(2,128)(2,1)S(1)}, bf16[512,2,2,128]{3,2,0,1:T(2,128)(2,1)S(1)}, u32[]{:S(2)}, u32[]{:S(2)}) collective-permute-start(bf16[512,2,2,128]{3,2,0,1:T(2,128)(2,1)S(1)} %constant_dynamic-update-slice_fusion), channel_id=1, source_target_pairs={{0,4},{4,8},{8,12},{12,16},{16,20},{20,24},{24,28},{28,32},{32,36}... | collective-permute-start | bytes 1572872 | tf_op jit(solution)/shard_map/ppermute | solution.py:19
  50.1 5.8 %collective-permute-done.2 = bf16[128,2,2,128]{3,2,1,0:T(2,128)(2,1)S(1)} collective-permute-done((bf16[128,2,2,128]{3,2,1,0:T(2,128)(2,1)S(1)}, bf16[128,2,2,128]{3,2,1,0:T(2,128)(2,1)S(1)}, u32[]{:S(2)}, u32[]{:S(2)}) %collective-permute-start.2) | collective-permute-done | bytes 131104 | tf_op jit(solution)/shard_map/ppermute | solution.py:25
  56.5 4.4 %collective-permute-start.3 = (bf16[256,2,2,128]{3,2,1,0:T(2,128)(2,1)S(1)}, bf16[256,2,2,128]{3,2,1,0:T(2,128)(2,1)S(1)}, u32[]{:S(2)}, u32[]{:S(2)}) collective-permute-start(bf16[256,2,2,128]{3,2,1,0:T(2,128)(2,1)S(1)} %broadcast_select_fusion.3), channel_id=1, source_target_pairs={{0,16},{4,20},{8,24},{12,28},{16,0},{20,4},{24,8},{28,12},{32,48},... | collective-permute-start | bytes 786440 | tf_op jit(solution)/shard_map/ppermute | solution.py:25
  60.9 1.3 fusion.60
  62.3 10.3 %collective-permute-done.3 = bf16[256,2,2,128]{3,2,1,0:T(2,128)(2,1)S(1)} collective-permute-done((bf16[256,2,2,128]{3,2,1,0:T(2,128)(2,1)S(1)}, bf16[256,2,2,128]{3,2,1,0:T(2,128)(2,1)S(1)}, u32[]{:S(2)}, u32[]{:S(2)}) %collective-permute-start.3) | collective-permute-done | bytes 262176 | tf_op jit(solution)/shard_map/ppermute | solution.py:25
  72.6 1.2 broadcast_select_fusion.2
  73.7 3.7 %collective-permute-start.4 = (bf16[512,2,2,128]{3,2,1,0:T(2,128)(2,1)S(1)}, bf16[512,2,2,128]{3,2,1,0:T(2,128)(2,1)}, u32[]{:S(2)}, u32[]{:S(2)}) collective-permute-start(bf16[512,2,2,128]{3,2,1,0:T(2,128)(2,1)S(1)} %broadcast_select_fusion.2), channel_id=1, source_target_pairs={{0,32},{4,36},{8,40},{12,44},{16,48},{20,52},{24,56},{28,60},{32,0... | collective-permute-start | bytes 1572872 | tf_op jit(solution)/shard_map/ppermute | solution.py:25
  77.5 4.7 %fusion.61 = (bf16[2,1024,128]{2,0,1:T(2,128)(2,1)S(1)}, bf16[2,1024,128]{2,0,1:T(2,128)(2,1)S(1)}) fusion(bf16[512,2,2,128]{3,2,0,1:T(2,128)(2,1)S(1)} %constant_dynamic-update-slice_fusion, bf16[512,2,2,128]{3,2,0,1:T(2,128)(2,1)S(1)} %collective-permute-done), kind=kLoop, calls=%fused_computation.89 | loop fusion | flops 524288 | bytes 2097152 | tf_op jit(solution)/shard_map/transpose | solution.py:45
  82.2 0.9 copy.36
  83.7 0.8 reshape.246
  84.5 16.9 %while.48 = (s32[]{:T(128)}, f32[2,512,4]{1,2,0:T(4,128)S(1)}, f32[2,512,4]{1,2,0:T(4,128)S(1)}, f32[2,512,4,128]{3,1,2,0:T(8,128)}, bf16[2,512,4,128]{3,2,0,1:T...) while((s32[]{:T(128)}, f32[2,512,4]{1,2,0:T(4,128)S(1)}, ...), condition=%wide.region_3.4_spmd.clone.clone, body=%wide.region_0.3_spmd.clone.sunk.clone | while | flops 1098903552 | bytes 49354956 | solution.py:50
  85.2 1.9 fusion.101
  87.0 2.4 %fusion.102 = f32[512,4]{0,1:T(4,128)S(1)} fusion(f32[512,4,1024]{2,0,1:T(8,128)S(1)} %get-tuple-element.523, f32[512,4]{0,1:T(4,128)S(1)} %get-tuple-element.524, pred[512,1024]{1,0:T(8,128)(4,1)S(1)} %fusion.100), kind=kLoop, calls=%fused_computation.7.clone.1.clone | loop fusion | flops 8386560 | bytes 8929280 | tf_op jit(solution)/shard_map/while/body/eval_jaxpr/reduce_sum | solution.py:36
  89.5 2.2 %fusion.103 = f32[2,512,4,128]{3,1,2,0:T(8,128)S(1)} fusion(f32[2,512,4,128]{3,1,2,0:T(8,128)S(1)} %copy-done, s32[]{:T(128)S(6)} %copy.90, f32[512,4,1024]{2,0,1:T(8,128)S(1)} %get-tuple-element.523, f32[512,4]{0,1:T(4,128)S(1)} %get-tuple-element.524, pred[512,1024]{1,0:T(8,128)(4,1)S(1)} %fusion.100, bf16[2,1024,128]{2,1,0:T(8,128)(2,1)S(1)} %copy-done.4), kind=kOutput, calls=%fused_computation.15.clone.1.clone | convolution fusion | flops 545259520 | bytes 10232832 | tf_op jit(solution)/shard_map/while/body/eval_jaxpr/agb,bd->agd/dot_general | solution.py:38
  91.7 1.3 copy-done.1
  93.6 1.9 fusion.101
  95.5 2.4 %fusion.102 = f32[512,4]{0,1:T(4,128)S(1)} fusion(f32[512,4,1024]{2,0,1:T(8,128)S(1)} %get-tuple-element.523, f32[512,4]{0,1:T(4,128)S(1)} %get-tuple-element.524, pred[512,1024]{1,0:T(8,128)(4,1)S(1)} %fusion.100), kind=kLoop, calls=%fused_computation.7.clone.1.clone | loop fusion | flops 8386560 | bytes 8929280 | tf_op jit(solution)/shard_map/while/body/eval_jaxpr/reduce_sum | solution.py:36
  97.9 2.2 %fusion.103 = f32[2,512,4,128]{3,1,2,0:T(8,128)S(1)} fusion(f32[2,512,4,128]{3,1,2,0:T(8,128)S(1)} %copy-done, s32[]{:T(128)S(6)} %copy.90, f32[512,4,1024]{2,0,1:T(8,128)S(1)} %get-tuple-element.523, f32[512,4]{0,1:T(4,128)S(1)} %get-tuple-element.524, pred[512,1024]{1,0:T(8,128)(4,1)S(1)} %fusion.100, bf16[2,1024,128]{2,1,0:T(8,128)(2,1)S(1)} %copy-done.4), kind=kOutput, calls=%fused_computation.15.clone.1.clone | convolution fusion | flops 545259520 | bytes 10232832 | tf_op jit(solution)/shard_map/while/body/eval_jaxpr/agb,bd->agd/dot_general | solution.py:38
  100.1 1.3 copy-done.1
  101.4 0.7 reshape_reshape.7
  102.2 0.9 select_reduce_fusion.1
  103.1 0.6 select_reduce_fusion
  103.7 3.6 %broadcast_select_fusion = bf16[1024,2,2,128]{3,2,1,0:T(2,128)(2,1)S(1)} fusion(pred[]{:T(512)S(6)} %eq.122, bf16[512,2,2,128]{3,2,1,0:T(2,128)(2,1)S(1)} %broadcast_select_fusion.2, bf16[512,2,2,128]{3,2,1,0:T(2,128)(2,1)} %collective-permute-done.4), kind=kLoop, calls=%fused_computation.75 | loop fusion | flops 1572864 | bytes 2097153 | tf_op jit(solution)/shard_map/jit(_where)/select_n | solution.py:79
  107.4 0.7 slice_bitcast_fusion.2
  108.3 2.5 %while.49 = (s32[]{:T(128)}, f32[2,64,4]{1,2,0:T(4,128)S(1)}, f32[2,64,4]{1,2,0:T(4,128)S(1)}, f32[2,64,4,128]{3,1,2,0:T(8,128)S(1)}, bf16[2,64,4,128]{3,2,0,1:T...) while((s32[]{:T(128)}, f32[2,64,4]{1,2,0:T(4,128)S(1)}, ...), condition=%wide.region_9.10_spmd.clone.clone, body=%wide.region_6.9_spmd.clone.sunk.clone | while | flops 136117760 | bytes 4143465 | solution.py:50
  111.5 63.3 %all-gather.2.cloned.1.call-done = bf16[1024,2,2,128]{3,2,0,1:T(2,128)(2,1)} async-done(((bf16[8,2,2,128]{3,2,0,1:T(2,128)(2,1)}), bf16[1024,2,2,128]{3,2,0,1:T(2,128)(2,1)}) %all-gather.2.cloned.1.call-update) | async-done | bytes 1048592 | tf_op jit(solution)/shard_map/all_gather | solution.py:124
  174.8 1.9 slice_bitcast_fusion
  176.9 1.6 while.50
  178.9 3.1 %fusion.58 = bf16[2,512,4,128]{3,1,2,0:T(8,128)(2,1)S(1)} fusion(f32[2,512,4,128]{3,1,2,0:T(8,128)S(1)} %copy-done.2, f32[2,512,4]{1,2,0:T(4,128)S(1)} %get-tuple-element.307, f32[2,8,4,128]{3,1,2,0:T(8,128)S(1)} %get-tuple-element.142, f32[2,512,4]{1,2,0:T(4,128)S(1)} %get-tuple-element.310, f32[2,64,4,128]{3,1,2,0:T(8,128)S(1)} %get-tuple-element.141, ...), kind=kLoop, calls=%fused_computation.74 | loop fusion | flops 4718592 | bytes 3508224 | tf_op jit(solution)/shard_map/convert_element_type | solution.py:142
  182.0 0.8 copy.49
  182.9 0.8 all_to_all.59
  183.6 19.8 %all_to_all.67 = bf16[4,128,1024]{2,1,0:T(8,128)(2,1)S(1)} all-to-all(bf16[4,128,1024]{2,1,0:T(8,128)(2,1)S(1)} %all_to_all.59), channel_id=1, replica_groups=mesh['ctx'=128,'tensor'=4] {'tensor'}, dimensions={0} | all-to-all | bytes 2097152 | tf_op jit(solution)/shard_map/all_to_all | solution.py:144
  203.4 0.7 copy.50
  204.1 1.3 copy.51
  (121 shorter events, 10.7 us)
Async XLA Ops:
  6.5 18.9 %copy-start.17 = (s32[2]{0:T(128)S(1)}, s32[2]{0:T(128)}, u32[]{:S(2)}) copy-start(s32[2]{0:T(128)} %param.15) | copy-start | bytes 28
  6.5 17.6 %copy-start.3 = (bf16[128,4096]{1,0:T(8,128)(2,1)S(1)}, bf16[128,4096]{1,0:T(8,128)(2,1)}, u32[]{:S(2)}) copy-start(bf16[128,4096]{1,0:T(8,128)(2,1)} %param.11) | copy-start | bytes 3145732
  8.4 20.6 %copy-start.18 = (s32[2]{0:T(128)S(1)}, s32[2]{0:T(128)}, u32[]{:S(2)}) copy-start(s32[2]{0:T(128)} %param.14) | copy-start | bytes 28
  8.4 17.0 %all-to-all-start.1 = ((bf16[128,4,256]{0,2,1:T(8,128)(2,1)}), bf16[128,4,256]{0,2,1:T(8,128)(2,1)S(1)}, u32[]{:S(2)}, u32[]{:S(2)}) async-start(bf16[128,4,256]{0,2,1:T(8,128)(2,1)} %bitcast.3), calls=%async_computation.1 | async-start | bytes 524288 | tf_op jit(solution)/shard_map/all_to_all | solution.py:87
  25.5 8.7 %all-to-all-start.2 = ((bf16[128,4,256]{0,2,1:T(8,128)(2,1)}), bf16[128,4,256]{0,2,1:T(8,128)(2,1)S(1)}, u32[]{:S(2)}, u32[]{:S(2)}) async-start(bf16[128,4,256]{0,2,1:T(8,128)(2,1)} %bitcast.5), calls=%async_computation.2 | async-start | bytes 524288 | tf_op jit(solution)/shard_map/all_to_all | solution.py:88
  29.1 9.6 %copy-start.15 = (pred[8,2]{0,1:T(4,128)(4,1)}, pred[8,2]{0,1:T(4,128)(4,1)S(1)}, u32[]{:S(2)}) copy-start(pred[8,2]{0,1:T(4,128)(4,1)S(1)} %iota_compare_fusion.7) | copy-start | bytes 52
  34.2 49.0 %all-to-all-start = ((bf16[128,4,1024]{0,2,1:T(8,128)(2,1)}), bf16[128,4,1024]{0,2,1:T(8,128)(2,1)S(1)}, u32[]{:S(2)}, u32[]{:S(2)}) async-start(bf16[128,4,1024]{0,2,1:T(8,128)(2,1)} %bitcast), calls=%async_computation | async-start | bytes 2097152 | tf_op jit(solution)/shard_map/all_to_all | solution.py:86
  38.5 136.2 %all-gather.2.cloned.1.call-start = ((), (), s32[]{:S(2)}) async-start(), calls=%async_computation.4 | async-start | bytes 1056768 | tf_op jit(solution)/shard_map/all_gather | solution.py:124
  39.2 5.5 %collective-permute-start.1 = (bf16[64,2,2,128]{3,2,1,0:T(2,128)(2,1)S(1)}, bf16[64,2,2,128]{3,2,1,0:T(2,128)(2,1)S(1)}, u32[]{:S(2)}, u32[]{:S(2)}) collective-permute-start(bf16[64,2,2,128]{3,2,1,0:T(2,128)(2,1)S(1)} %fusion.62), channel_id=1, source_target_pairs={{0,4},{4,0},{8,12},{12,8},{16,20},{20,16},{24,28},{28,24},{32,36},... | collective-permute-start | bytes 196616 | tf_op jit(solution)/shard_map/ppermute | solution.py:25
  45.0 10.9 %collective-permute-start.2 = (bf16[128,2,2,128]{3,2,1,0:T(2,128)(2,1)S(1)}, bf16[128,2,2,128]{3,2,1,0:T(2,128)(2,1)S(1)}, u32[]{:S(2)}, u32[]{:S(2)}) collective-permute-start(bf16[128,2,2,128]{3,2,1,0:T(2,128)(2,1)S(1)} %broadcast_select_fusion.4), channel_id=1, source_target_pairs={{0,8},{4,12},{8,0},{12,4},{16,24},{20,28},{24,16},{28,20},{32,40},... | collective-permute-start | bytes 393224 | tf_op jit(solution)/shard_map/ppermute | solution.py:25
  47.6 29.9 %collective-permute-start = (bf16[512,2,2,128]{3,2,0,1:T(2,128)(2,1)S(1)}, bf16[512,2,2,128]{3,2,0,1:T(2,128)(2,1)S(1)}, u32[]{:S(2)}, u32[]{:S(2)}) collective-permute-start(bf16[512,2,2,128]{3,2,0,1:T(2,128)(2,1)S(1)} %constant_dynamic-update-slice_fusion), channel_id=1, source_target_pairs={{0,4},{4,8},{8,12},{12,16},{16,20},{20,24},{24,28},{28,32},{32,36}... | collective-permute-start | bytes 1572872 | tf_op jit(solution)/shard_map/ppermute | solution.py:19
  56.5 16.0 %collective-permute-start.3 = (bf16[256,2,2,128]{3,2,1,0:T(2,128)(2,1)S(1)}, bf16[256,2,2,128]{3,2,1,0:T(2,128)(2,1)S(1)}, u32[]{:S(2)}, u32[]{:S(2)}) collective-permute-start(bf16[256,2,2,128]{3,2,1,0:T(2,128)(2,1)S(1)} %broadcast_select_fusion.3), channel_id=1, source_target_pairs={{0,16},{4,20},{8,24},{12,28},{16,0},{20,4},{24,8},{28,12},{32,48},... | collective-permute-start | bytes 786440 | tf_op jit(solution)/shard_map/ppermute | solution.py:25
  73.7 30.0 %collective-permute-start.4 = (bf16[512,2,2,128]{3,2,1,0:T(2,128)(2,1)S(1)}, bf16[512,2,2,128]{3,2,1,0:T(2,128)(2,1)}, u32[]{:S(2)}, u32[]{:S(2)}) collective-permute-start(bf16[512,2,2,128]{3,2,1,0:T(2,128)(2,1)S(1)} %broadcast_select_fusion.2), channel_id=1, source_target_pairs={{0,32},{4,36},{8,40},{12,44},{16,48},{20,52},{24,56},{28,60},{32,0... | collective-permute-start | bytes 1572872 | tf_op jit(solution)/shard_map/ppermute | solution.py:25
  87.0 2.4 %copy-start = (f32[2,512,4,128]{3,1,2,0:T(8,128)S(1)}, f32[2,512,4,128]{3,1,2,0:T(8,128)}, u32[]{:S(2)}) copy-start(f32[2,512,4,128]{3,1,2,0:T(8,128)} %get-tuple-element.595) | copy-start | bytes 6291460 | tf_op jit(solution)/shard_map/while
  87.0 2.4 %copy-start.4 = (bf16[2,1024,128]{2,1,0:T(8,128)(2,1)S(1)}, bf16[2,1024,128]{2,1,0:T(8,128)(2,1)}, u32[]{:S(2)}) copy-start(bf16[2,1024,128]{2,1,0:T(8,128)(2,1)} %get-tuple-element.608) | copy-start | bytes 1572868 | tf_op jit(solution)/shard_map/while
  91.7 1.3 copy-start.1
  95.5 2.4 %copy-start = (f32[2,512,4,128]{3,1,2,0:T(8,128)S(1)}, f32[2,512,4,128]{3,1,2,0:T(8,128)}, u32[]{:S(2)}) copy-start(f32[2,512,4,128]{3,1,2,0:T(8,128)} %get-tuple-element.595) | copy-start | bytes 6291460 | tf_op jit(solution)/shard_map/while
  95.5 2.4 %copy-start.4 = (bf16[2,1024,128]{2,1,0:T(8,128)(2,1)S(1)}, bf16[2,1024,128]{2,1,0:T(8,128)(2,1)}, u32[]{:S(2)}) copy-start(bf16[2,1024,128]{2,1,0:T(8,128)(2,1)} %get-tuple-element.608) | copy-start | bytes 1572868 | tf_op jit(solution)/shard_map/while
  100.1 1.3 copy-start.1
  101.4 0.8 copy-start.16
  107.3 1.0 copy-start.5
  107.3 0.9 copy-start.9
  107.4 0.9 copy-start.11
  107.4 0.9 copy-start.12
  111.4 65.4 %copy-start.6 = (f32[2,8,4,128]{3,1,2,0:T(8,128)S(1)}, f32[2,8,4,128]{3,1,2,0:T(8,128)}, u32[]{:S(2)}) copy-start(f32[2,8,4,128]{3,1,2,0:T(8,128)} %custom-call.6) | copy-start | bytes 98308
  111.4 65.4 %copy-start.10 = (s32[8]{0:T(128)S(1)}, s32[8]{0:T(128)}, u32[]{:S(2)}) copy-start(s32[8]{0:T(128)} %iota_add_fusion.1) | copy-start | bytes 100
  111.4 65.4 %copy-start.13 = (f32[2,8,4]{1,2,0:T(4,128)S(1)}, f32[2,8,4]{1,2,0:T(4,128)}, u32[]{:S(2)}) copy-start(f32[2,8,4]{1,2,0:T(4,128)} %custom-call.5) | copy-start | bytes 772
  111.5 65.4 %copy-start.14 = (f32[2,8,4]{1,2,0:T(4,128)S(1)}, f32[2,8,4]{1,2,0:T(4,128)}, u32[]{:S(2)}) copy-start(f32[2,8,4]{1,2,0:T(4,128)} %custom-call.4) | copy-start | bytes 772
  176.8 2.2 %copy-start.2 = (f32[2,512,4,128]{3,1,2,0:T(8,128)S(1)}, f32[2,512,4,128]{3,1,2,0:T(8,128)}, u32[]{:S(2)}) copy-start(f32[2,512,4,128]{3,1,2,0:T(8,128)} %get-tuple-element.140) | copy-start | bytes 6291460
  176.9 2.0 copy-start.7
  176.9 2.0 copy-start.8
Sparse Core Ops, SparseCore 0:
  62.4 112.3 all-gather.1
where the time goes:
time: 213 us; the launch traced here: 212 us
  waiting for transfers between devices  87.4 us (41%)
  starting transfers between devices  32.8 us (15%)
  other arithmetic  26.3 us (12%)
  local copies, waits for them, and re-layouts  20.9 us (10%)
  blocking collectives  19.8 us (9%)
  between operations  14 us (7%)
  matrix products  10.7 us (5%)
    all_gather x1, waiting for transfers between devices, on_device(): far_all = lax.all_gather(far_kv, 'ctx', axis=0, tiled=True)  63.3 us
    all_to_all x1, blocking collectives, on_device(): lax.all_to_all(attended, 'tensor', split_axis=0, concat_axis=1, tiled=True)  19.8 us
    ppermute x4, waiting for transfers between devices, partner_2(): return lax.ppermute(value, axis, pairs)  19.2 us
    ppermute x4, starting transfers between devices, partner_2(): return lax.ppermute(value, axis, pairs)  12 us
    all_to_all x1, starting transfers between devices, on_device(): lax.all_to_all(keys, 'tensor', split_axis=1, concat_axis=0, tiled=True)  10.4 us
    unnamed x42, local copies, waits for them, and re-layouts  6.5 us
    reduce_sum x6, other arithmetic, head_stats(): totals = jnp.sum(powers, axis=-1)  5.78 us
    select_n x4, other arithmetic, join_halves(): jnp.where(upper_half, jnp.concatenate([partner, mine], 0), jnp.concatenat...  5.62 us
  transfers between devices with their start and end apart: 9, of which 5 were waited for; matrix products, arithmetic and copies ran while one was open for 20% of the time, Pallas kernels for 0%

commit v1 on v0

--- a/solution.py
+++ b/solution.py
@@ -1,6 +1,8 @@
 import jax
 import jax.numpy as jnp
 from jax import lax
+from jax.experimental import pallas as pl
+from jax.experimental.pallas import tpu as pltpu
 from jax.sharding import PartitionSpec as P
 
 HEADS = 32
@@ -13,16 +15,147 @@
 NEG_FILL = -1e30
 
 
-def passed_along(value, axis, steps):
-    count = lax.axis_size(axis)
-    leading, last = (max(0, -steps), min(count, count - steps))
-    return lax.ppermute(value, axis, [(source, source + steps) for source in range(leading, last)])
-
-
-def partner_2(value, axis, stride):
-    mask = 2**stride
-    pairs = [(source, source ^ mask) for source in range(lax.axis_size(axis))]
-    return lax.ppermute(value, axis, pairs)
+RING = 8
+MESH_IDS = pl.DeviceIdType.MESH
+
+
+def exchange_body(
+    kv_ref, mid_ref, fk_ref, fv_ref,
+    prev_out, mid_out, fk_out, fv_out,
+    local_sem, prev_sem, x_send, x_recv, mid_send, mid_recv, fwd_send, fwd_recv,
+    k1_send, k1_recv, v1_send, v1_recv, k2_send, k2_recv, v2_send, v2_recv,
+):
+    place = lax.axis_index("ctx")
+    total = 2 * RING * RING
+    z = lax.rem(place, RING)
+    y = lax.rem(place // RING, RING)
+    x = place // (RING * RING)
+
+    def at(xi, yi, zi):
+        return {"ctx": (xi * RING + yi) * RING + zi}
+
+    def z_peer(step):
+        return at(x, y, lax.rem(z + step, RING))
+
+    def y_peer(step):
+        return at(x, lax.rem(y + step, RING), z)
+
+    x_peer = at(1 - x, y, z)
+    parity = lax.rem(y, 2)
+    y_pair = at(x, y + 1 - 2 * parity, z)
+    after = {"ctx": lax.rem(place + 1, total)}
+    before = {"ctx": lax.rem(place + total - 1, total)}
+
+    barrier = pltpu.get_barrier_semaphore()
+    greeted = [x_peer, after, before]
+    greeted += [z_peer(step) for step in range(1, RING)]
+    greeted += [y_peer(step) for step in range(1, RING)]
+    for peer in greeted:
+        pl.semaphore_signal(barrier, inc=1, device_id=peer, device_id_type=MESH_IDS)
+    pl.semaphore_wait(barrier, len(greeted))
+
+    def remote(source, target, send, recv, peer):
+        copy = pltpu.make_async_remote_copy(
+            src_ref=source, dst_ref=target, send_sem=send, recv_sem=recv,
+            device_id=peer, device_id_type=MESH_IDS,
+        )
+        copy.start()
+        return copy
+
+    own_k = pltpu.make_async_copy(fk_ref, fk_out.at[y, z, x], local_sem.at[0])
+    own_v = pltpu.make_async_copy(fv_ref, fv_out.at[z, y, x], local_sem.at[1])
+    own_mid = pltpu.make_async_copy(mid_ref, mid_out.at[parity, z], local_sem.at[2])
+    own_k.start()
+    own_v.start()
+    own_mid.start()
+    x_k = remote(fk_ref, fk_out.at[y, z, x], x_send.at[0], x_recv.at[0], x_peer)
+    x_v = remote(fv_ref, fv_out.at[z, y, x], x_send.at[1], x_recv.at[1], x_peer)
+    order = [4, 3, 5, 2, 6, 1, 7]
+    mids = {
+        step: remote(
+            mid_ref, mid_out.at[parity, z], mid_send.at[step], mid_recv.at[step], z_peer(step)
+        )
+        for step in order
+    }
+    forwards = [
+        remote(mid_ref, mid_out.at[parity, z], fwd_send.at[0], fwd_recv.at[0], y_pair)
+    ]
+    own_k.wait()
+    own_v.wait()
+    x_k.wait_recv()
+    x_v.wait_recv()
+    firsts_k = {
+        step: remote(
+            fk_out.at[y, z], fk_out.at[y, z], k1_send.at[step], k1_recv.at[step], z_peer(step)
+        )
+        for step in order
+    }
+    firsts_v = {
+        step: remote(
+            fv_out.at[z, y], fv_out.at[z, y], v1_send.at[step], v1_recv.at[step], y_peer(step)
+        )
+        for step in order
+    }
+    ahead = remote(kv_ref, prev_out, prev_sem.at[0], prev_sem.at[1], after)
+    for step in order:
+        firsts_v[step].wait_recv()
+    seconds_v = {
+        step: remote(fv_out.at[z], fv_out.at[z], v2_send.at[step], v2_recv.at[step], z_peer(step))
+        for step in order
+    }
+    for step in order:
+        firsts_k[step].wait_recv()
+    seconds_k = {
+        step: remote(fk_out.at[y], fk_out.at[y], k2_send.at[step], k2_recv.at[step], y_peer(step))
+        for step in order
+    }
+    for step in [1, 7, 2, 6, 3, 5, 4]:
+        mids[step].wait_recv()
+        source = lax.rem(z + RING - step, RING)
+        forwards.append(
+            remote(
+                mid_out.at[parity, source], mid_out.at[parity, source],
+                fwd_send.at[step], fwd_recv.at[step], y_pair,
+            )
+        )
+    for copy in forwards:
+        copy.wait_recv()
+    for step in order:
+        seconds_k[step].wait_recv()
+        seconds_v[step].wait_recv()
+    ahead.wait()
+    own_mid.wait()
+    x_k.wait_send()
+    x_v.wait_send()
+    for step in order:
+        for group in (mids, firsts_k, firsts_v, seconds_k, seconds_v):
+            group[step].wait_send()
+    for copy in forwards:
+        copy.wait_send()
+
+
+def exchange(kv_rows, mid_kv, far_k, far_v):
+    sems = [pltpu.SemaphoreType.DMA((RING,)) for _ in range(12)]
+    return pl.pallas_call(
+        exchange_body,
+        out_shape=[
+            jax.ShapeDtypeStruct(kv_rows.shape, jnp.bfloat16),
+            jax.ShapeDtypeStruct((2, RING) + mid_kv.shape, jnp.bfloat16),
+            jax.ShapeDtypeStruct((RING, RING, 2) + far_k.shape, jnp.bfloat16),
+            jax.ShapeDtypeStruct((RING, RING, 2) + far_v.shape, jnp.bfloat16),
+        ],
+        in_specs=[pl.BlockSpec(memory_space=pltpu.VMEM)] * 4,
+        out_specs=[pl.BlockSpec(memory_space=pltpu.VMEM)] * 4,
+        scratch_shapes=[
+            pltpu.SemaphoreType.DMA((3,)),
+            pltpu.SemaphoreType.DMA((2,)),
+            pltpu.SemaphoreType.DMA((2,)),
+            pltpu.SemaphoreType.DMA((2,)),
+        ]
+        + sems,
+        compiler_params=pltpu.CompilerParams(collective_id=0, has_side_effects=True),
+        name="exchange",
+    )(kv_rows, mid_kv, far_k, far_v)
 
 
 def head_stats(query_rows, key_rows, value_rows, allowed, scale_factor):
@@ -75,33 +208,40 @@
     return (maxima, totals, weighted.reshape(kv_local, -1, per_group, weighted.shape[-1]))
 
 
-def join_halves(mine, partner, upper_half):
-    return jnp.where(
-        upper_half, jnp.concatenate([partner, mine], 0), jnp.concatenate([mine, partner], 0)
-    )
-
-
 def on_device(queries, keys, values, mid_offsets, far_offsets):
-    queries, keys, values = (
-        lax.all_to_all(queries, "tensor", split_axis=1, concat_axis=0, tiled=True),
-        lax.all_to_all(keys, "tensor", split_axis=1, concat_axis=0, tiled=True),
-        lax.all_to_all(values, "tensor", split_axis=1, concat_axis=0, tiled=True),
-    )
+    count = lax.axis_size("tensor")
+    own = queries.shape[0]
+    kv_rows = jnp.concatenate(
+        [keys.reshape(own, count, -1), values.reshape(own, count, -1)], axis=2
+    ).reshape(own, -1)
+    kv_rows = lax.all_to_all(kv_rows, "tensor", split_axis=1, concat_axis=0, tiled=True)
+    queries = lax.all_to_all(queries, "tensor", split_axis=1, concat_axis=0, tiled=True)
     tok_rows = queries.shape[0]
     kv_local = mid_offsets.shape[0]
     per_group = HEADS // KV_HEADS
     scale_factor = HEAD_DIM ** (-0.5)
     query_rows = queries.reshape(tok_rows, kv_local, per_group, HEAD_DIM)
-    kv_rows = jnp.stack(
-        [keys.reshape(tok_rows, kv_local, HEAD_DIM), values.reshape(tok_rows, kv_local, HEAD_DIM)],
-        axis=1,
-    )
     ctx_count = lax.axis_size("ctx")
     ctx_place = lax.axis_index("ctx")
     team_size = min(16, ctx_count)
-    team_bits = team_size.bit_length() - 1
-    previous = passed_along(kv_rows, "ctx", 1)
-    near_keys = jnp.concatenate([previous, kv_rows], 0)
+    kv_dims = (2, kv_local, HEAD_DIM)
+    kv_heads = kv_rows.reshape((tok_rows,) + kv_dims)
+    mid_kv = pick_rows(kv_heads, mid_offsets, RATE_MID, 2)
+    far_kv = pick_rows(kv_heads, far_offsets, RATE_FAR, 2)
+    mid_count = tok_rows // RATE_MID
+    far_count = tok_rows // RATE_FAR
+    far_flat = far_kv.transpose(1, 2, 0, 3).reshape(2, kv_local * far_count, HEAD_DIM)
+    previous, mid_all, far_k, far_v = exchange(
+        kv_rows, mid_kv.reshape(mid_count, -1), far_flat[0], far_flat[1]
+    )
+    mid_all = mid_all.reshape((team_size * mid_count,) + kv_dims)
+    far_split = (RING, RING, 2, kv_local, far_count, HEAD_DIM)
+    far_k = far_k.reshape(far_split).transpose(3, 2, 0, 1, 4, 5)
+    far_v = far_v.reshape(far_split).transpose(3, 2, 1, 0, 4, 5)
+    far_all = jnp.stack(
+        [far_k.reshape(kv_local, -1, HEAD_DIM), far_v.reshape(kv_local, -1, HEAD_DIM)]
+    ).transpose(2, 0, 1, 3)
+    near_keys = jnp.concatenate([previous, kv_rows], 0).reshape((-1,) + kv_dims)
     query_index = jnp.arange(tok_rows)[:, None]
     key_index = jnp.arange(2 * tok_rows)[None, :]
     near_allowed = jnp.where(
@@ -111,17 +251,7 @@
     )
     near_stats = branch_stats(query_rows, near_keys, near_allowed, scale_factor)
     mid_queries = pick_rows(query_rows, mid_offsets, RATE_MID, 1)
-    mid_kv = pick_rows(kv_rows, mid_offsets, RATE_MID, 2)
     far_queries = pick_rows(query_rows, far_offsets, RATE_FAR, 1)
-    far_kv = pick_rows(kv_rows, far_offsets, RATE_FAR, 2)
-    mid_count = tok_rows // RATE_MID
-    far_count = tok_rows // RATE_FAR
-    mid_all = mid_kv
-    for bit_index in range(team_bits):
-        upper_half = ctx_place // (1 << bit_index) % 2 == 1
-        partner = partner_2(mid_all, "ctx", bit_index)
-        mid_all = join_halves(mid_all, partner, upper_half)
-    far_all = lax.all_gather(far_kv, "ctx", axis=0, tiled=True)
     mid_position = ctx_place % team_size * mid_count + jnp.arange(mid_count)[:, None]
     mid_allowed = jnp.arange(team_size * mid_count)[None, :] <= mid_position
     mid_stats = spread_stats(

time: 213 us -> 157 us (0.74)
  waiting for transfers between devices: 87.4 us -> 3.87 us
  Pallas kernels: 0 us -> 61.2 us
  starting transfers between devices: 32.8 us -> 14.7 us
  between operations: 14 us -> 0.43 us
  other arithmetic: 26.3 us -> 21 us
  local copies, waits for them, and re-layouts: 20.9 us -> 25.2 us
  blocking collectives: 19.8 us -> 17 us
    all_gather x1 -> x0, waiting for transfers between devices: 63.3 us -> none  [on_device(): far_all = lax.all_gather(far_kv, 'ctx', axis=0, tiled=True)]
    pallas_call x0 -> x1, Pallas kernels: none -> 61.2 us  [exchange(): pl.pallas_call(exchange_body, out_shape=[jax.ShapeDtypeStruct(kv_rows.sha...]
    ppermute x5 -> x0, waiting for transfers between devices: 19.2 us -> none  [the longest x4 19.2 us: partner_2(): return lax.ppermute(value, axis, pairs)]
    ppermute x5 -> x0, starting transfers between devices: 14.5 us -> none  [the longest x4 12 us: partner_2(): return lax.ppermute(value, axis, pairs)]
    select_n x4 -> x0, other arithmetic: 5.62 us -> none  [join_halves(): jnp.where(upper_half, jnp.concatenate([partner, mine], 0), jnp.concatenat...]
    transpose x1, other arithmetic: 4.74 us -> 0.1 us  [on_device(): far_all = jnp.stack([far_k.reshape(kv_local, -1, HEAD_DIM), far_v.reshape...]
    all_to_all x2 -> x1, starting transfers between devices: 13.9 us -> 10.3 us  [on_device(): lax.all_to_all(kv_rows, 'tensor', split_axis=1, concat_axis=0, tiled=True)]
    reshape x0 -> x3, local copies, waits for them, and re-layouts: none -> 3.15 us  [the longest x1 1.35 us: on_device(): mid_all = mid_all.reshape((team_size * mid_count,) + kv_dims)]
  transfers between devices with their start and end apart: 9 -> 2, of which waited for: 5 -> 1; matrix products, arithmetic and copies ran while one was open for 20% -> 10% of each run, Pallas kernels for 0% -> 39%
where the time goes in v1:
time: 157 us
  Pallas kernels  61.2 us (39%)
  local copies, waits for them, and re-layouts  25.2 us (16%)
  other arithmetic  21 us (13%)
  blocking collectives  17 us (11%)
  starting transfers between devices  14.7 us (9%)
  matrix products  12.6 us (8%)
  waiting for transfers between devices  3.87 us (2%)
    pallas_call x1, Pallas kernels, exchange(): pl.pallas_call(exchange_body, out_shape=[jax.ShapeDtypeStruct(kv_rows.sha...  61.2 us
    all_to_all x1, blocking collectives, on_device(): lax.all_to_all(attended, 'tensor', split_axis=0, concat_axis=1, tiled=True)  17 us
    all_to_all x1, starting transfers between devices, on_device(): lax.all_to_all(kv_rows, 'tensor', split_axis=1, concat_axis=0, tiled=True)  10.3 us
    dot_general x6, matrix products, head_stats(): jnp.einsum('agd,bd->agb', query_rows, key_rows, preferred_element_type=jn...  7.01 us
    convert_element_type x1, other arithmetic, on_device(): attended = (numerator / denominator[..., None]).astype(jnp.bfloat16)  5.84 us
    reduce_sum x6, other arithmetic, head_stats(): totals = jnp.sum(powers, axis=-1)  5.75 us
    dot_general x6, matrix products, head_stats(): jnp.einsum('agb,bd->agd', weights, value_rows, preferred_element_type=jnp...  5.59 us
    reduce_sum x4, other arithmetic, pick_rows(): return jnp.sum(kept, axis=1)  4.56 us
  transfers between devices with their start and end apart: 2, of which 1 were waited for; matrix products, arithmetic and copies ran while one was open for 10% of the time, Pallas kernels for 39%

profile of v1, /device:TPU:1, one launch (start us, length us, event | category | flops | bytes accessed | tf_op | source)
XLA Modules:
  0.0 156.6 jit_solution(1078988553208996276)
XLA Ops:
  0.0 1.2 copy_bitcast_fusion.8
  1.2 0.8 pad_maximum_fusion
  2.0 10.3 %all-to-all-start.1 = ((bf16[128,4,512]{2,0,1:T(8,128)(2,1)}), bf16[128,4,512]{2,0,1:T(8,128)(2,1)S(1)}, u32[]{:S(2)}, u32[]{:S(2)}) async-start(bf16[128,4,512]{2,0,1:T(8,128)(2,1)} %pad_maximum_fusion), calls=%async_computation.1 | async-start | bytes 1048576 | tf_op jit(solution)/shard_map/all_to_all | solution.py:217
  12.4 0.6 iota_add_fusion.2
  13.0 1.3 copy.40
  14.9 0.7 broadcast_in_dim.307
  15.7 0.7 broadcast_in_dim.316
  16.5 3.9 %all-to-all-done.1 = bf16[128,4,512]{2,0,1:T(8,128)(2,1)S(1)} async-done(((bf16[128,4,512]{2,0,1:T(8,128)(2,1)}), bf16[128,4,512]{2,0,1:T(8,128)(2,1)S(1)}, u32[]{:S(2)}, u32[]{:S(2)}) %all-to-all-start.1) | async-done | bytes 524320 | tf_op jit(solution)/shard_map/all_to_all | solution.py:217
  20.3 4.4 %all-to-all-start = ((bf16[128,4,1024]{0,2,1:T(8,128)(2,1)}), bf16[128,4,1024]{0,2,1:T(8,128)(2,1)S(1)}, u32[]{:S(2)}, u32[]{:S(2)}) async-start(bf16[128,4,1024]{0,2,1:T(8,128)(2,1)} %bitcast), calls=%async_computation | async-start | bytes 2097152 | tf_op jit(solution)/shard_map/all_to_all | solution.py:218
  24.9 0.6 fusion.59
  25.6 0.6 copy.87
  26.2 0.6 copy.88
  27.3 0.7 reshape.265.mid_ref
  28.0 61.2 %exchange.1 = (bf16[512,512]{1,0:T(8,128)(2,1)}, bf16[2,8,64,512]{3,2,1,0:T(8,128)(2,1)}, bf16[8,8,2,16,128]{4,3,2,1,0:T(8,128)(2,1)}, bf16[8,8,2,16,128]{4,3,2,1,0:T(8,128)(2,1)}) custom-call(bf16[512,512]{1,0:T(8,128)(2,1)} %bitcast.219, bf16[64,512]{1,0:T(8,128)(2,1)} %reshape.265.mid_ref, bf16[16,128]{1,0:T(8,128)(2,1)} %bitcast.237, ...), custom_call_target="tpu_custom_call" | custom-call | tf_op jit(solution)/shard_map/exchange/pallas_call | solution.py:139
  89.2 1.3 reshape.266
  90.6 0.7 fusion.62
  91.4 0.9 copy.86
  92.4 1.0 copy.55
  93.4 1.2 concatenate.12
  95.3 0.7 slice_bitcast_fusion.2
  96.1 0.9 copy.48
  97.1 1.1 slice_bitcast_fusion
  98.7 1.5 reshape_reshape.15
  100.2 0.7 reshape.262
  101.0 1.5 select_reduce_fusion.1
  102.5 7.0 %while.49 = (s32[]{:T(128)}, f32[2,64,4]{1,2,0:T(4,128)}, f32[2,64,4]{1,2,0:T(4,128)}, f32[2,64,4,128]{3,1,2,0:T(8,128)S(1)}, bf16[2,64,4,128]{3,2,0,1:T(4,128)(...) while((s32[]{:T(128)}, f32[2,64,4]{1,2,0:T(4,128)}, ...), condition=%wide.region_10.11_spmd.clone.clone, body=%wide.region_7.10_spmd.clone.sunk.clone | while | flops 136117760 | bytes 4176845 | solution.py:183
  102.6 0.8 iota_compare_fusion.13
  103.4 1.3 fusion.104
  105.5 0.6 copy-done.15
  106.1 0.8 iota_compare_fusion.13
  106.9 1.3 fusion.104
  109.6 0.9 broadcast_in_dim.312
  110.6 0.8 broadcast_in_dim.329
  111.6 1.9 %select_reduce_fusion = bf16[8,2,4,128]{3,2,1,0:T(4,128)(2,1)S(1)} fusion(bf16[8,64,2,4,128]{4,3,2,1,0:T(4,128)(2,1)} %reshape_reshape.15, pred[64,2]{1,0:T(8,128)(4,1)S(1)} %iota_compare_fusion.4), kind=kLoop, calls=%fused_computation.76 | loop fusion | flops 1040384 | bytes 1065088 | tf_op jit(solution)/shard_map/reduce_sum | solution.py:193
  113.6 1.6 %while.50 = (s32[]{:T(128)}, f32[2,8,4]{1,2,0:T(4,128)S(1)}, f32[2,8,4]{1,2,0:T(4,128)S(1)}, f32[2,8,4,128]{3,1,2,0:T(8,128)S(1)}, bf16[2,8,4,128]{3,2,0,1:T(4,1...) while((s32[]{:T(128)}, f32[2,8,4]{1,2,0:T(4,128)S(1)}, ...), condition=%wide.region_15.16_spmd.clone.clone, body=%wide.region_12.15_spmd.clone.sunk.clone | while | flops 17014720 | bytes 986625 | solution.py:183
  115.6 14.5 %while.48 = (s32[]{:T(128)}, f32[2,512,4]{1,2,0:T(4,128)S(1)}, f32[2,512,4]{1,2,0:T(4,128)S(1)}, f32[2,512,4,128]{3,1,2,0:T(8,128)}, bf16[2,512,4,128]{3,2,0,1:T...) while((s32[]{:T(128)}, f32[2,512,4]{1,2,0:T(4,128)S(1)}, ...), condition=%wide.region_5.6_spmd.clone.clone, body=%wide.region_2.5_spmd.clone.sunk.clone | while | flops 1098903552 | bytes 47257768 | solution.py:183
  116.4 1.9 %fusion.99 = (f32[512,4]{0,1:T(4,128)S(1)}, f32[512,4,1024]{2,0,1:T(8,128)S(1)}) fusion(pred[512,1024]{1,0:T(8,128)(4,1)S(1)} %fusion.98, bf16[2,1024,128]{2,1,0:T(8,128)(2,1)S(1)} %get-tuple-element.619, s32[]{:T(128)} %get-tuple-element.604, bf16[1,512,4,128]{3,2,0,1:T(4,128)(2,1)S(1)} %constant_dynamic-slice_fusion.9), kind=kOutput, calls=%fused_computation.5.clone.1.clone | convolution fusion | flops 543160320 | bytes 9707524 | tf_op jit(solution)/shard_map/while/body/eval_jaxpr/agd,bd->agb/dot_general | solution.py:163
  118.2 2.2 %fusion.101 = f32[2,512,4,128]{3,1,2,0:T(8,128)S(1)} fusion(f32[2,512,4,128]{3,1,2,0:T(8,128)S(1)} %copy-done.3, s32[]{:T(128)} %get-tuple-element.604, f32[512,4,1024]{2,0,1:T(8,128)S(1)} %get-tuple-element.535, f32[512,4]{0,1:T(4,128)S(1)} %get-tuple-element.536, pred[512,1024]{1,0:T(8,128)(4,1)S(1)} %fusion.98, ...), kind=kOutput, calls=%fused_computation.15.clone.1.clone | convolution fusion | flops 545259520 | bytes 10232832 | tf_op jit(solution)/shard_map/while/body/eval_jaxpr/agb,bd->agd/dot_general | solution.py:171
  120.5 2.4 %fusion.100 = f32[512,4]{0,1:T(4,128)S(1)} fusion(f32[512,4,1024]{2,0,1:T(8,128)S(1)} %get-tuple-element.535, f32[512,4]{0,1:T(4,128)S(1)} %get-tuple-element.536, pred[512,1024]{1,0:T(8,128)(4,1)S(1)} %fusion.98), kind=kLoop, calls=%fused_computation.7.clone.1.clone | loop fusion | flops 8386560 | bytes 8929280 | tf_op jit(solution)/shard_map/while/body/eval_jaxpr/reduce_sum | solution.py:169
  123.5 1.9 %fusion.99 = (f32[512,4]{0,1:T(4,128)S(1)}, f32[512,4,1024]{2,0,1:T(8,128)S(1)}) fusion(pred[512,1024]{1,0:T(8,128)(4,1)S(1)} %fusion.98, bf16[2,1024,128]{2,1,0:T(8,128)(2,1)S(1)} %get-tuple-element.619, s32[]{:T(128)} %get-tuple-element.604, bf16[1,512,4,128]{3,2,0,1:T(4,128)(2,1)S(1)} %constant_dynamic-slice_fusion.9), kind=kOutput, calls=%fused_computation.5.clone.1.clone | convolution fusion | flops 543160320 | bytes 9707524 | tf_op jit(solution)/shard_map/while/body/eval_jaxpr/agd,bd->agb/dot_general | solution.py:163
  125.4 2.2 %fusion.101 = f32[2,512,4,128]{3,1,2,0:T(8,128)S(1)} fusion(f32[2,512,4,128]{3,1,2,0:T(8,128)S(1)} %copy-done.3, s32[]{:T(128)} %get-tuple-element.604, f32[512,4,1024]{2,0,1:T(8,128)S(1)} %get-tuple-element.535, f32[512,4]{0,1:T(4,128)S(1)} %get-tuple-element.536, pred[512,1024]{1,0:T(8,128)(4,1)S(1)} %fusion.98, ...), kind=kOutput, calls=%fused_computation.15.clone.1.clone | convolution fusion | flops 545259520 | bytes 10232832 | tf_op jit(solution)/shard_map/while/body/eval_jaxpr/agb,bd->agd/dot_general | solution.py:171
  127.6 2.4 %fusion.100 = f32[512,4]{0,1:T(4,128)S(1)} fusion(f32[512,4,1024]{2,0,1:T(8,128)S(1)} %get-tuple-element.535, f32[512,4]{0,1:T(4,128)S(1)} %get-tuple-element.536, pred[512,1024]{1,0:T(8,128)(4,1)S(1)} %fusion.98), kind=kLoop, calls=%fused_computation.7.clone.1.clone | loop fusion | flops 8386560 | bytes 8929280 | tf_op jit(solution)/shard_map/while/body/eval_jaxpr/reduce_sum | solution.py:169
  130.1 5.8 %fusion.58 = bf16[2,512,4,128]{3,1,2,0:T(8,128)(2,1)S(1)} fusion(f32[2,512,4,128]{3,1,2,0:T(8,128)} %get-tuple-element.148, f32[2,512,4]{1,2,0:T(4,128)S(1)} %get-tuple-element.315, f32[2,8,4,128]{3,1,2,0:T(8,128)S(1)} %get-tuple-element.150, f32[2,512,4]{1,2,0:T(4,128)S(1)} %get-tuple-element.318, f32[2,64,4,128]{3,1,2,0:T(8,128)S(1)} %get-tuple-element.149, ...), kind=kLoop, calls=%fused_computation.74 | loop fusion | flops 4718592 | bytes 3508224 | tf_op jit(solution)/shard_map/convert_element_type | solution.py:272
  136.0 0.8 copy.57
  136.8 0.8 all_to_all.44
  137.5 17.0 %all_to_all.51 = bf16[4,128,1024]{2,1,0:T(8,128)(2,1)S(1)} all-to-all(bf16[4,128,1024]{2,1,0:T(8,128)(2,1)S(1)} %all_to_all.44), channel_id=1, replica_groups=mesh['ctx'=128,'tensor'=4] {'tensor'}, dimensions={0} | all-to-all | bytes 2097152 | tf_op jit(solution)/shard_map/all_to_all | solution.py:274
  154.6 0.7 copy.58
  155.2 1.3 copy.59
  (120 shorter events, 8.9 us)
Async XLA Ops:
  0.0 13.0 %copy-start.6 = (bf16[128,4096]{1,0:T(8,128)(2,1)S(1)}, bf16[128,4096]{1,0:T(8,128)(2,1)}, u32[]{:S(2)}) copy-start(bf16[128,4096]{1,0:T(8,128)(2,1)} %param.11) | copy-start | bytes 3145732
  1.2 13.7 %copy-start.22 = (s32[2]{0:T(128)S(1)}, s32[2]{0:T(128)}, u32[]{:S(2)}) copy-start(s32[2]{0:T(128)} %param.14) | copy-start | bytes 28
  1.2 14.4 %copy-start.21 = (s32[2]{0:T(128)S(1)}, s32[2]{0:T(128)}, u32[]{:S(2)}) copy-start(s32[2]{0:T(128)} %param.15) | copy-start | bytes 28
  2.0 18.3 %all-to-all-start.1 = ((bf16[128,4,512]{2,0,1:T(8,128)(2,1)}), bf16[128,4,512]{2,0,1:T(8,128)(2,1)S(1)}, u32[]{:S(2)}, u32[]{:S(2)}) async-start(bf16[128,4,512]{2,0,1:T(8,128)(2,1)} %pad_maximum_fusion), calls=%async_computation.1 | async-start | bytes 1048576 | tf_op jit(solution)/shard_map/all_to_all | solution.py:217
  16.4 10.3 %copy-start.20 = (pred[8,2]{0,1:T(4,128)(4,1)}, pred[8,2]{0,1:T(4,128)(4,1)S(1)}, u32[]{:S(2)}) copy-start(pred[8,2]{0,1:T(4,128)(4,1)S(1)} %iota_compare_fusion.8) | copy-start | bytes 52
  20.3 6.5 %copy-start = (bf16[128,4,512]{2,0,1:T(8,128)(2,1)}, bf16[128,4,512]{2,0,1:T(8,128)(2,1)S(1)}, u32[]{:S(2)}) copy-start(bf16[128,4,512]{2,0,1:T(8,128)(2,1)S(1)} %all-to-all-done.1) | copy-start | bytes 1572868
  20.3 77.8 %all-to-all-start = ((bf16[128,4,1024]{0,2,1:T(8,128)(2,1)}), bf16[128,4,1024]{0,2,1:T(8,128)(2,1)S(1)}, u32[]{:S(2)}, u32[]{:S(2)}) async-start(bf16[128,4,1024]{0,2,1:T(8,128)(2,1)} %bitcast), calls=%async_computation | async-start | bytes 2097152 | tf_op jit(solution)/shard_map/all_to_all | solution.py:218
  90.6 1.7 %copy-start.9 = (bf16[8,8,2,16,128]{4,3,2,1,0:T(8,128)(2,1)S(1)}, bf16[8,8,2,16,128]{4,3,2,1,0:T(8,128)(2,1)}, u32[]{:S(2)}) copy-start(bf16[8,8,2,16,128]{4,3,2,1,0:T(8,128)(2,1)} %get-tuple-element.145) | copy-start | bytes 1572868
  91.3 1.1 copy-start.8
  95.3 1.7 %copy-start.5 = (bf16[2,2,8,8,8,128]{5,4,3,2,1,0:T(8,128)(2,1)S(1)}, bf16[2,2,8,8,8,128]{5,4,3,2,1,0:T(8,128)(2,1)}, u32[]{:S(2)}) copy-start(bf16[2,2,8,8,8,128]{5,4,3,2,1,0:T(8,128)(2,1)} %copy.55) | copy-start | bytes 1572868
  102.5 2.9 %copy-start.14 = (f32[2,64,4]{1,2,0:T(4,128)S(1)}, f32[2,64,4]{1,2,0:T(4,128)}, u32[]{:S(2)}) copy-start(f32[2,64,4]{1,2,0:T(4,128)} %get-tuple-element.657) | copy-start | bytes 6148 | tf_op jit(solution)/shard_map/while
  102.5 2.9 %copy-start.16 = (f32[2,64,4]{1,2,0:T(4,128)S(1)}, f32[2,64,4]{1,2,0:T(4,128)}, u32[]{:S(2)}) copy-start(f32[2,64,4]{1,2,0:T(4,128)} %get-tuple-element.658) | copy-start | bytes 6148 | tf_op jit(solution)/shard_map/while
  105.5 0.6 copy-start.15
  105.5 0.6 copy-start.17
  106.1 2.9 %copy-start.14 = (f32[2,64,4]{1,2,0:T(4,128)S(1)}, f32[2,64,4]{1,2,0:T(4,128)}, u32[]{:S(2)}) copy-start(f32[2,64,4]{1,2,0:T(4,128)} %get-tuple-element.657) | copy-start | bytes 6148 | tf_op jit(solution)/shard_map/while
  106.1 2.9 %copy-start.16 = (f32[2,64,4]{1,2,0:T(4,128)S(1)}, f32[2,64,4]{1,2,0:T(4,128)}, u32[]{:S(2)}) copy-start(f32[2,64,4]{1,2,0:T(4,128)} %get-tuple-element.658) | copy-start | bytes 6148 | tf_op jit(solution)/shard_map/while
  108.9 0.6 copy-start.15
  109.0 0.6 copy-start.17
  109.5 3.9 %copy-start.1 = (bf16[2,1024,128]{2,1,0:T(8,128)(2,1)S(1)}, bf16[2,1024,128]{2,1,0:T(8,128)(2,1)}, u32[]{:S(2)}) copy-start(bf16[2,1024,128]{2,1,0:T(8,128)(2,1)} %get-tuple-element.629) | copy-start | bytes 1572868
  109.5 4.0 %copy-start.2 = (bf16[2,1024,128]{2,1,0:T(8,128)(2,1)S(1)}, bf16[2,1024,128]{2,1,0:T(8,128)(2,1)}, u32[]{:S(2)}) copy-start(bf16[2,1024,128]{2,1,0:T(8,128)(2,1)} %get-tuple-element.630) | copy-start | bytes 1572868
  109.6 4.0 %copy-start.10 = (f32[2,8,4,128]{3,1,2,0:T(8,128)S(1)}, f32[2,8,4,128]{3,1,2,0:T(8,128)}, u32[]{:S(2)}) copy-start(f32[2,8,4,128]{3,1,2,0:T(8,128)} %custom-call.6) | copy-start | bytes 98308
  109.6 4.0 %copy-start.13 = (s32[8]{0:T(128)S(1)}, s32[8]{0:T(128)}, u32[]{:S(2)}) copy-start(s32[8]{0:T(128)} %iota_add_fusion.1) | copy-start | bytes 100
  109.6 4.0 %copy-start.18 = (f32[2,8,4]{1,2,0:T(4,128)S(1)}, f32[2,8,4]{1,2,0:T(4,128)}, u32[]{:S(2)}) copy-start(f32[2,8,4]{1,2,0:T(4,128)} %custom-call.4) | copy-start | bytes 772
  109.6 4.0 %copy-start.19 = (f32[2,8,4]{1,2,0:T(4,128)S(1)}, f32[2,8,4]{1,2,0:T(4,128)}, u32[]{:S(2)}) copy-start(f32[2,8,4]{1,2,0:T(4,128)} %custom-call.5) | copy-start | bytes 772
  113.5 2.0 %copy-start.7 = (bf16[2,1024,128]{2,1,0:T(8,128)(2,1)S(1)}, bf16[2,1024,128]{2,1,0:T(8,128)(2,1)}, u32[]{:S(2)}) copy-start(bf16[2,1024,128]{2,1,0:T(8,128)(2,1)} %copy.48) | copy-start | bytes 1572868
  115.5 14.5 %copy-start.11 = (pred[2,512]{1,0:T(4,128)(4,1)S(1)}, pred[2,512]{1,0:T(4,128)(4,1)}, u32[]{:S(2)}) copy-start(pred[2,512]{1,0:T(4,128)(4,1)} %broadcast_in_dim.307) | copy-start | bytes 3076
  115.5 14.5 %copy-start.12 = (pred[2,512]{1,0:T(4,128)(4,1)S(1)}, pred[2,512]{1,0:T(4,128)(4,1)}, u32[]{:S(2)}) copy-start(pred[2,512]{1,0:T(4,128)(4,1)} %broadcast_in_dim.316) | copy-start | bytes 3076
  116.4 1.9 %copy-start.3 = (f32[2,512,4,128]{3,1,2,0:T(8,128)S(1)}, f32[2,512,4,128]{3,1,2,0:T(8,128)}, u32[]{:S(2)}) copy-start(f32[2,512,4,128]{3,1,2,0:T(8,128)} %get-tuple-element.607) | copy-start | bytes 6291460 | tf_op jit(solution)/shard_map/while
  120.4 2.4 %copy-start.4 = (f32[2,512,4,128]{3,1,2,0:T(8,128)}, f32[2,512,4,128]{3,1,2,0:T(8,128)S(1)}, u32[]{:S(2)}) copy-start(f32[2,512,4,128]{3,1,2,0:T(8,128)S(1)} %fusion.101) | copy-start | bytes 6291460 | tf_op jit(solution)/shard_map/while
  123.5 1.9 %copy-start.3 = (f32[2,512,4,128]{3,1,2,0:T(8,128)S(1)}, f32[2,512,4,128]{3,1,2,0:T(8,128)}, u32[]{:S(2)}) copy-start(f32[2,512,4,128]{3,1,2,0:T(8,128)} %get-tuple-element.607) | copy-start | bytes 6291460 | tf_op jit(solution)/shard_map/while
  127.6 2.4 %copy-start.4 = (f32[2,512,4,128]{3,1,2,0:T(8,128)}, f32[2,512,4,128]{3,1,2,0:T(8,128)S(1)}, u32[]{:S(2)}) copy-start(f32[2,512,4,128]{3,1,2,0:T(8,128)S(1)} %fusion.101) | copy-start | bytes 6291460 | tf_op jit(solution)/shard_map/while

commit v2 on v1

--- a/solution.py
+++ b/solution.py
@@ -19,14 +19,23 @@
 MESH_IDS = pl.DeviceIdType.MESH
 
 
+CHUNK = 128
+
+
 def exchange_body(
-    kv_ref, mid_ref, fk_ref, fv_ref,
-    prev_out, mid_out, fk_out, fv_out,
-    local_sem, prev_sem, x_send, x_recv, mid_send, mid_recv, fwd_send, fwd_recv,
+    q_ref, kv_ref, mid_ref, fk_ref, fv_ref,
+    q_out, prev_out, mid_out, fk_out, fv_out, near_out, max_out, sum_out,
+    local_sem, prev_send, prev_recv, q_send, q_recv, x_send, x_recv,
+    mid_send, mid_recv, fwd_send, fwd_recv,
     k1_send, k1_recv, v1_send, v1_recv, k2_send, k2_recv, v2_send, v2_recv,
 ):
     place = lax.axis_index("ctx")
+    lane = lax.axis_index("tensor")
     total = 2 * RING * RING
+    lanes = q_out.shape[0]
+    width = q_out.shape[2]
+    kv_local = kv_ref.shape[1] // (2 * HEAD_DIM)
+    per_group = width // (kv_local * HEAD_DIM)
     z = lax.rem(place, RING)
     y = lax.rem(place // RING, RING)
     x = place // (RING * RING)
@@ -35,10 +44,10 @@
         return {"ctx": (xi * RING + yi) * RING + zi}
 
     def z_peer(step):
-        return at(x, y, lax.rem(z + step, RING))
+        return at(x, y, lax.rem(z + RING + step, RING))
 
     def y_peer(step):
-        return at(x, lax.rem(y + step, RING), z)
+        return at(x, lax.rem(y + RING + step, RING), z)
 
     x_peer = at(1 - x, y, z)
     parity = lax.rem(y, 2)
@@ -50,6 +59,7 @@
     greeted = [x_peer, after, before]
     greeted += [z_peer(step) for step in range(1, RING)]
     greeted += [y_peer(step) for step in range(1, RING)]
+    greeted += [{"tensor": lax.rem(lane + step, lanes)} for step in range(1, lanes)]
     for peer in greeted:
         pl.semaphore_signal(barrier, inc=1, device_id=peer, device_id_type=MESH_IDS)
     pl.semaphore_wait(barrier, len(greeted))
@@ -62,24 +72,75 @@
         copy.start()
         return copy
 
+    def columns(index):
+        return pl.ds(pl.multiple_of(index * width, width), width)
+
+    class Ring:
+        def __init__(self, block, place_in, peer, send, recv, own, hops):
+            self.block, self.place, self.peer = block, place_in, peer
+            self.send, self.recv, self.own, self.hops = send, recv, own, hops
+            self.sent = {}
+
+        def source(self, way, step):
+            return lax.rem(self.place + 2 * RING - way * step, RING)
+
+        def start(self, step):
+            for slot, way in ((0, 1), (1, -1)):
+                if step > self.hops[slot]:
+                    continue
+                target = self.block(self.source(way, step - 1))
+                origin = target
+                if step == 1 and self.own is not None:
+                    origin = self.own
+                index = slot * RING + step
+                self.sent[slot, step] = remote(
+                    origin, target, self.send.at[index], self.recv.at[index], self.peer(way)
+                )
+
+        def landed(self, step):
+            found = []
+            for slot, way in ((0, 1), (1, -1)):
+                if step <= self.hops[slot]:
+                    self.sent[slot, step].wait_recv()
+                    found.append((slot * RING + step, self.block(self.source(way, step))))
+            return found
+
+        def finish(self):
+            for copy in self.sent.values():
+                copy.wait_send()
+
     own_k = pltpu.make_async_copy(fk_ref, fk_out.at[y, z, x], local_sem.at[0])
     own_v = pltpu.make_async_copy(fv_ref, fv_out.at[z, y, x], local_sem.at[1])
     own_mid = pltpu.make_async_copy(mid_ref, mid_out.at[parity, z], local_sem.at[2])
-    own_k.start()
-    own_v.start()
-    own_mid.start()
+    own_q = pltpu.make_async_copy(q_ref.at[:, columns(lane)], q_out.at[lane], local_sem.at[3])
+    for copy in (own_k, own_v, own_mid, own_q):
+        copy.start()
     x_k = remote(fk_ref, fk_out.at[y, z, x], x_send.at[0], x_recv.at[0], x_peer)
     x_v = remote(fv_ref, fv_out.at[z, y, x], x_send.at[1], x_recv.at[1], x_peer)
-    order = [4, 3, 5, 2, 6, 1, 7]
-    mids = {
-        step: remote(
-            mid_ref, mid_out.at[parity, z], mid_send.at[step], mid_recv.at[step], z_peer(step)
-        )
-        for step in order
-    }
+    mid_ring = Ring(
+        lambda i: mid_out.at[parity, i], z, z_peer, mid_send, mid_recv, mid_ref, (3, 4)
+    )
+    mid_ring.start(1)
     forwards = [
         remote(mid_ref, mid_out.at[parity, z], fwd_send.at[0], fwd_recv.at[0], y_pair)
     ]
+    moves = []
+    for step in range(1, lanes):
+        other = lax.rem(lane + step, lanes)
+        moves.append(
+            remote(
+                q_ref.at[:, columns(other)], q_out.at[lane],
+                q_send.at[step], q_recv.at[step], {"tensor": other},
+            )
+        )
+    chunks = kv_ref.shape[0] // CHUNK
+    ahead = {}
+    for chunk in reversed(range(chunks)):
+        rows = pl.ds(chunk * CHUNK, CHUNK)
+        ahead[chunk] = remote(
+            kv_ref.at[rows], prev_out.at[rows], prev_send.at[chunk], prev_recv.at[chunk], after
+        )
+    order = [4, 3, 5, 2, 6, 1, 7]
     own_k.wait()
     own_v.wait()
     x_k.wait_recv()
@@ -96,66 +157,134 @@
         )
         for step in order
     }
-    ahead = remote(kv_ref, prev_out, prev_sem.at[0], prev_sem.at[1], after)
-    for step in order:
-        firsts_v[step].wait_recv()
-    seconds_v = {
-        step: remote(fv_out.at[z], fv_out.at[z], v2_send.at[step], v2_recv.at[step], z_peer(step))
-        for step in order
-    }
+
+    def mid_step(step):
+        for index, block in mid_ring.landed(step - 1):
+            forwards.append(
+                remote(block, block, fwd_send.at[index], fwd_recv.at[index], y_pair)
+            )
+        if step <= 4:
+            mid_ring.start(step)
+
+    mid_step(2)
     for step in order:
         firsts_k[step].wait_recv()
-    seconds_k = {
-        step: remote(fk_out.at[y], fk_out.at[y], k2_send.at[step], k2_recv.at[step], y_peer(step))
-        for step in order
-    }
-    for step in [1, 7, 2, 6, 3, 5, 4]:
-        mids[step].wait_recv()
-        source = lax.rem(z + RING - step, RING)
-        forwards.append(
-            remote(
-                mid_out.at[parity, source], mid_out.at[parity, source],
-                fwd_send.at[step], fwd_recv.at[step], y_pair,
+        firsts_v[step].wait_recv()
+    k_ring = Ring(lambda i: fk_out.at[i], y, y_peer, k2_send, k2_recv, None, (3, 4))
+    v_ring = Ring(lambda i: fv_out.at[i], z, z_peer, v2_send, v2_recv, None, (3, 4))
+    k_ring.start(1)
+    v_ring.start(1)
+
+    def near(chunk):
+        first = chunk * CHUNK
+        span = kv_ref.shape[0] + CHUNK
+        row = lax.broadcasted_iota(jnp.int32, (CHUNK, span), 0)
+        col = lax.broadcasted_iota(jnp.int32, (CHUNK, span), 1)
+        allowed = (col > row) & (col <= row + kv_ref.shape[0])
+        allowed = allowed & ((col >= kv_ref.shape[0] - first) | (place > 0))
+        bias = jnp.where(allowed, 0.0, NEG_FILL)
+        bias = jnp.concatenate([bias] * per_group, 0)
+
+        @pl.loop(0, kv_local)
+        def _(head):
+            def window(part):
+                cols = pl.ds(
+                    pl.multiple_of((part * kv_local + head) * HEAD_DIM, HEAD_DIM), HEAD_DIM
+                )
+                return jnp.concatenate(
+                    [prev_out[first:, cols], kv_ref[: first + CHUNK, cols]], 0
+                )
+
+            group = per_group * HEAD_DIM
+            wide = q_out[chunk, :, pl.ds(pl.multiple_of(head * group, group), group)]
+            rows = jnp.concatenate(
+                [wide[:, g * HEAD_DIM : (g + 1) * HEAD_DIM] for g in range(per_group)], 0
             )
-        )
+            scores = lax.dot_general(
+                rows, window(0), (((1,), (1,)), ((), ())), preferred_element_type=jnp.float32
+            )
+            scores = scores * HEAD_DIM ** (-0.5) + bias
+            maxima = jnp.max(scores, axis=1, keepdims=True)
+            powers = jnp.exp(scores - maxima)
+            totals = jnp.sum(powers, axis=1, keepdims=True)
+            weighted = jnp.dot(
+                powers.astype(jnp.bfloat16), window(1), preferred_element_type=jnp.float32
+            )
+            for g in range(per_group):
+                mine = slice(g * CHUNK, (g + 1) * CHUNK)
+                near_out[head * per_group + g, first : first + CHUNK] = weighted[mine]
+                max_out[head * per_group + g, first : first + CHUNK] = maxima[mine]
+                sum_out[head * per_group + g, first : first + CHUNK] = totals[mine]
+
+    mid_step(3)
+    k_ring.landed(1)
+    k_ring.start(2)
+    v_ring.landed(1)
+    v_ring.start(2)
+    own_q.wait()
+    ahead[3].wait_recv()
+    for copy in moves:
+        copy.wait_recv()
+    near(3)
+    mid_step(4)
+    k_ring.landed(2)
+    k_ring.start(3)
+    v_ring.landed(2)
+    v_ring.start(3)
+    ahead[2].wait_recv()
+    near(2)
+    mid_step(5)
+    k_ring.landed(3)
+    k_ring.start(4)
+    v_ring.landed(3)
+    v_ring.start(4)
+    ahead[1].wait_recv()
+    near(1)
+    ahead[0].wait_recv()
+    near(0)
+    k_ring.landed(4)
+    v_ring.landed(4)
     for copy in forwards:
         copy.wait_recv()
-    for step in order:
-        seconds_k[step].wait_recv()
-        seconds_v[step].wait_recv()
-    ahead.wait()
     own_mid.wait()
     x_k.wait_send()
     x_v.wait_send()
     for step in order:
-        for group in (mids, firsts_k, firsts_v, seconds_k, seconds_v):
-            group[step].wait_send()
-    for copy in forwards:
+        firsts_k[step].wait_send()
+        firsts_v[step].wait_send()
+    for copy in forwards + moves + list(ahead.values()):
         copy.wait_send()
-
-
-def exchange(kv_rows, mid_kv, far_k, far_v):
-    sems = [pltpu.SemaphoreType.DMA((RING,)) for _ in range(12)]
+    for ring in (mid_ring, k_ring, v_ring):
+        ring.finish()
+
+
+def exchange(queries, kv_rows, mid_kv, far_k, far_v):
+    lanes = lax.axis_size("tensor")
+    own, wide = queries.shape
+    rows = kv_rows.shape[0]
+    heads = HEADS // lanes
+    sizes = [4, 4, 4, 4, 4, 2, 2] + [2 * RING] * 12
+    stat = jax.ShapeDtypeStruct((heads, rows, 1), jnp.float32)
     return pl.pallas_call(
         exchange_body,
         out_shape=[
+            jax.ShapeDtypeStruct((lanes, own, wide // lanes), jnp.bfloat16),
             jax.ShapeDtypeStruct(kv_rows.shape, jnp.bfloat16),
             jax.ShapeDtypeStruct((2, RING) + mid_kv.shape, jnp.bfloat16),
             jax.ShapeDtypeStruct((RING, RING, 2) + far_k.shape, jnp.bfloat16),
             jax.ShapeDtypeStruct((RING, RING, 2) + far_v.shape, jnp.bfloat16),
+            jax.ShapeDtypeStruct((heads, rows, HEAD_DIM), jnp.float32),
+            stat,
+            stat,
         ],
-        in_specs=[pl.BlockSpec(memory_space=pltpu.VMEM)] * 4,
-        out_specs=[pl.BlockSpec(memory_space=pltpu.VMEM)] * 4,
-        scratch_shapes=[
-            pltpu.SemaphoreType.DMA((3,)),
-            pltpu.SemaphoreType.DMA((2,)),
-            pltpu.SemaphoreType.DMA((2,)),
-            pltpu.SemaphoreType.DMA((2,)),
-        ]
-        + sems,
-        compiler_params=pltpu.CompilerParams(collective_id=0, has_side_effects=True),
+        in_specs=[pl.BlockSpec(memory_space=pltpu.VMEM)] * 5,
+        out_specs=[pl.BlockSpec(memory_space=pltpu.VMEM)] * 8,
+        scratch_shapes=[pltpu.SemaphoreType.DMA((size,)) for size in sizes],
+        compiler_params=pltpu.CompilerParams(
+            collective_id=0, has_side_effects=True, vmem_limit_bytes=48 * 2**20
+        ),
         name="exchange",
-    )(kv_rows, mid_kv, far_k, far_v)
+    )(queries, kv_rows, mid_kv, far_k, far_v)
 
 
 def head_stats(query_rows, key_rows, value_rows, allowed, scale_factor):
@@ -215,12 +344,10 @@
         [keys.reshape(own, count, -1), values.reshape(own, count, -1)], axis=2
     ).reshape(own, -1)
     kv_rows = lax.all_to_all(kv_rows, "tensor", split_axis=1, concat_axis=0, tiled=True)
-    queries = lax.all_to_all(queries, "tensor", split_axis=1, concat_axis=0, tiled=True)
-    tok_rows = queries.shape[0]
+    tok_rows = kv_rows.shape[0]
     kv_local = mid_offsets.shape[0]
     per_group = HEADS // KV_HEADS
     scale_factor = HEAD_DIM ** (-0.5)
-    query_rows = queries.reshape(tok_rows, kv_local, per_group, HEAD_DIM)
     ctx_count = lax.axis_size("ctx")
     ctx_place = lax.axis_index("ctx")
     team_size = min(16, ctx_count)
@@ -231,8 +358,8 @@
     mid_count = tok_rows // RATE_MID
     far_count = tok_rows // RATE_FAR
     far_flat = far_kv.transpose(1, 2, 0, 3).reshape(2, kv_local * far_count, HEAD_DIM)
-    previous, mid_all, far_k, far_v = exchange(
-        kv_rows, mid_kv.reshape(mid_count, -1), far_flat[0], far_flat[1]
+    gathered, _, mid_all, far_k, far_v, *near = exchange(
+        queries, kv_rows, mid_kv.reshape(mid_count, -1), far_flat[0], far_flat[1]
     )
     mid_all = mid_all.reshape((team_size * mid_count,) + kv_dims)
     far_split = (RING, RING, 2, kv_local, far_count, HEAD_DIM)
@@ -241,15 +368,9 @@
     far_all = jnp.stack(
         [far_k.reshape(kv_local, -1, HEAD_DIM), far_v.reshape(kv_local, -1, HEAD_DIM)]
     ).transpose(2, 0, 1, 3)
-    near_keys = jnp.concatenate([previous, kv_rows], 0).reshape((-1,) + kv_dims)
-    query_index = jnp.arange(tok_rows)[:, None]
-    key_index = jnp.arange(2 * tok_rows)[None, :]
-    near_allowed = jnp.where(
-        key_index >= tok_rows,
-        key_index - tok_rows <= query_index,
-        (key_index > query_index) & (ctx_place > 0),
-    )
-    near_stats = branch_stats(query_rows, near_keys, near_allowed, scale_factor)
+    query_rows = gathered.reshape(tok_rows, kv_local, per_group, HEAD_DIM)
+    near = [part.reshape(kv_local, per_group, tok_rows, -1).transpose(0, 2, 1, 3) for part in near]
+    near_stats = (near[1][..., 0], near[2][..., 0], near[0])
     mid_queries = pick_rows(query_rows, mid_offsets, RATE_MID, 1)
     far_queries = pick_rows(query_rows, far_offsets, RATE_FAR, 1)
     mid_position = ctx_place % team_size * mid_count + jnp.arange(mid_count)[:, None]

time: 157 us -> 121 us (0.77)
  Pallas kernels: 61.2 us -> 47.5 us
  matrix products: 12.6 us -> 2.54 us
  local copies, waits for them, and re-layouts: 25.2 us -> 17.4 us
  starting transfers between devices: 14.7 us -> 10.3 us
  waiting for transfers between devices: 3.87 us -> 6.02 us
  other arithmetic: 21 us -> 19.1 us
    pallas_call x1, Pallas kernels: 61.2 us -> 47.5 us  [exchange(): pl.pallas_call(exchange_body, out_shape=[jax.ShapeDtypeStruct((lanes, own...]
    dot_general x6 -> x4, matrix products: 7.01 us -> 1.37 us  [head_stats(): jnp.einsum('agd,bd->agb', query_rows, key_rows, preferred_element_type=jn...]
    reduce_sum x6 -> x4, other arithmetic: 5.75 us -> 0.99 us  [head_stats(): totals = jnp.sum(powers, axis=-1)]
    dot_general x6 -> x4, matrix products: 5.59 us -> 1.17 us  [head_stats(): jnp.einsum('agb,bd->agd', weights, value_rows, preferred_element_type=jnp...]
    pallas_call x0 -> x2, other arithmetic: none -> 4.4 us  [exchange(): pl.pallas_call(exchange_body, out_shape=[jax.ShapeDtypeStruct((lanes, own...]
    all_to_all x1 -> x0, starting transfers between devices: 4.36 us -> none  [on_device(): lax.all_to_all(queries, 'tensor', split_axis=1, concat_axis=0, tiled=True)]
    mul x0 -> x3, local copies, waits for them, and re-layouts: none -> 3.09 us  [on_device(): numerator = numerator + factor[..., None] * stats[2]]
    convert_element_type x1, other arithmetic: 5.84 us -> 8.33 us  [on_device(): attended = (numerator / denominator[..., None]).astype(jnp.bfloat16)]
  transfers between devices with their start and end apart: 2 -> 1, of which waited for: 1 -> 1; matrix products, arithmetic and copies ran while one was open for 10% -> 2% of each run, Pallas kernels for 39% -> 0%
where the time goes in v2:
time: 121 us; the launch traced here: 120 us
  Pallas kernels  47.5 us (39%)
  other arithmetic  19.1 us (16%)
  local copies, waits for them, and re-layouts  17.4 us (14%)
  blocking collectives  16.7 us (14%)
  starting transfers between devices  10.3 us (9%)
  waiting for transfers between devices  6.02 us (5%)
  matrix products  2.54 us (2%)
    pallas_call x1, Pallas kernels, exchange(): pl.pallas_call(exchange_body, out_shape=[jax.ShapeDtypeStruct((lanes, own...  47.5 us
    all_to_all x1, blocking collectives, on_device(): lax.all_to_all(attended, 'tensor', split_axis=0, concat_axis=1, tiled=True)  16.7 us
    all_to_all x1, starting transfers between devices, on_device(): lax.all_to_all(kv_rows, 'tensor', split_axis=1, concat_axis=0, tiled=True)  10.3 us
    convert_element_type x1, other arithmetic, on_device(): attended = (numerator / denominator[..., None]).astype(jnp.bfloat16)  8.33 us
    all_to_all x1, waiting for transfers between devices, on_device(): lax.all_to_all(kv_rows, 'tensor', split_axis=1, concat_axis=0, tiled=True)  6.02 us
    pallas_call x2, other arithmetic, exchange(): pl.pallas_call(exchange_body, out_shape=[jax.ShapeDtypeStruct((lanes, own...  4.4 us
    mul x3, local copies, waits for them, and re-layouts, on_device(): numerator = numerator + factor[..., None] * stats[2]  3.09 us
    unnamed x36, local copies, waits for them, and re-layouts  3 us
  transfers between devices with their start and end apart: 1, of which 1 were waited for; matrix products, arithmetic and copies ran while one was open for 2% of the time, Pallas kernels for 0%

profile of v2, /device:TPU:1, one launch (start us, length us, event | category | flops | bytes accessed | tf_op | source)
XLA Modules:
  0.0 120.2 jit_solution(12714547797809670215)
XLA Ops:
  0.0 1.1 copy_bitcast_fusion.6
  1.1 0.8 pad_maximum_fusion
  1.9 10.3 %all-to-all-start = ((bf16[128,4,512]{2,0,1:T(8,128)(2,1)}), bf16[128,4,512]{2,0,1:T(8,128)(2,1)S(1)}, u32[]{:S(2)}, u32[]{:S(2)}) async-start(bf16[128,4,512]{2,0,1:T(8,128)(2,1)} %pad_maximum_fusion), calls=%async_computation | async-start | bytes 1048576 | tf_op jit(solution)/shard_map/all_to_all | solution.py:346
  12.3 0.5 iota_add_fusion.1
  12.8 0.6 iota_add_fusion
  13.7 0.2 copy.62
  13.9 0.2 copy.65
  14.2 6.0 %all-to-all-done = bf16[128,4,512]{2,0,1:T(8,128)(2,1)S(1)} async-done(((bf16[128,4,512]{2,0,1:T(8,128)(2,1)}), bf16[128,4,512]{2,0,1:T(8,128)(2,1)S(1)}, u32[]{:S(2)}, u32[]{:S(2)}) %all-to-all-start) | async-done | bytes 524320 | tf_op jit(solution)/shard_map/all_to_all | solution.py:346
  20.2 0.5 select_reduce_fusion.2
  21.0 0.6 fusion.32
  21.6 47.5 %exchange.1 = (bf16[4,128,1024]{2,1,0:T(8,128)(2,1)S(1)}, bf16[512,512]{1,0:T(8,128)(2,1)}, bf16[2,8,64,512]{3,2,1,0:T(8,128)(2,1)S(1)}, bf16[8,8,2,16,128]{4,3,...) custom-call(bf16[128,4096]{1,0:T(8,128)(2,1)S(1)} %copy-done, ...), custom_call_target="tpu_custom_call" | custom-call | tf_op jit(solution)/shard_map/exchange/pallas_call | solution.py:268
  69.2 1.0 copy-done.1
  70.2 0.8 copy-done.3
  71.0 2.2 %reduce.4 = f32[8,512]{1,0:T(8,128)S(1)} reduce(f32[8,512,1]{2,1,0:T(8,128)} %get-tuple-element.100, f32[]{:T(128)} %constant.88), dimensions={2}, to_apply=%get-tuple-element.100.reduce_sub_computation | reduce | bytes 32772 | tf_op jit(solution)/shard_map/exchange/pallas_call | solution.py:268
  73.2 2.2 %reduce.5 = f32[8,512]{1,0:T(8,128)S(1)} reduce(f32[8,512,1]{2,1,0:T(8,128)} %get-tuple-element.110, f32[]{:T(128)} %constant.88), dimensions={2}, to_apply=%get-tuple-element.110.reduce_sub_computation | reduce | bytes 32772 | tf_op jit(solution)/shard_map/exchange/pallas_call | solution.py:268
  75.5 1.6 %reshape_reshape.15 = bf16[8,64,2,4,128]{4,3,2,1,0:T(4,128)(2,1)} reshape(bf16[4,128,1024]{2,1,0:T(8,128)(2,1)S(1)} %get-tuple-element.101) | data formatting | bytes 2097152 | tf_op jit(solution)/shard_map/reshape;reshape | solution.py:316
  77.0 0.9 select_reduce_fusion.1
  78.4 1.0 copy-done.2
  79.4 0.3 reshape.292
  79.7 0.7 fusion.42
  80.6 4.2 %while.30 = (s32[]{:T(128)}, f32[2,64,4]{1,2,0:T(4,128)S(1)}, f32[2,64,4]{1,2,0:T(4,128)S(1)}, f32[2,64,4,128]{3,2,0,1:T(4,128)}, bf16[2,64,4,128]{3,2,0,1:T(4,1...) while((s32[]{:T(128)}, f32[2,64,4]{1,2,0:T(4,128)S(1)}, ...), condition=%wide.region_6.7_spmd.clone, body=%wide.region_3.6_spmd.clone.sunk | while | flops 136117760 | bytes 6501809 | solution.py:312
  80.8 0.4 fusion.54
  81.2 0.3 fusion.55
  81.5 0.4 convolution_bitcast_fusion.4
  82.1 0.7 copy-done.8
  82.9 0.4 fusion.54
  83.3 0.3 fusion.55
  83.6 0.4 convolution_bitcast_fusion.4
  84.2 0.7 copy-done.8
  85.0 0.2 broadcast_in_dim.309
  85.3 0.2 broadcast_in_dim.310
  85.5 0.6 select_reduce_fusion
  86.2 1.7 %while.31 = (s32[]{:T(128)}, f32[2,8,4]{1,2,0:T(4,128)S(1)}, f32[2,8,4]{1,2,0:T(4,128)S(1)}, f32[2,8,4,128]{3,2,0,1:T(4,128)S(1)}, bf16[2,8,4,128]{3,2,0,1:T(4,1...) while((s32[]{:T(128)}, f32[2,8,4]{1,2,0:T(4,128)S(1)}, ...), condition=%wide.region_11.12_spmd.clone, body=%wide.region_8.11_spmd.clone.sunk | while | flops 17014720 | bytes 1018393 | solution.py:312
  86.3 0.3 fusion.58
  86.6 0.2 fusion.59
  86.7 0.2 convolution_bitcast_fusion.5
  87.1 0.3 fusion.58
  87.4 0.2 fusion.59
  87.6 0.2 convolution_bitcast_fusion.5
  88.3 1.0 copy.74
  89.4 1.0 copy.71
  90.4 1.0 copy.73
  91.4 1.0 copy.72
  92.5 8.3 %fusion.31 = bf16[2,512,4,128]{3,2,0,1:T(4,128)(2,1)S(1)} fusion(f32[2,4,512,128]{3,2,1,0:T(8,128)S(1)} %bitcast.190, f32[2,512,4]{2,0,1:T(2,128)} %bitcast.191, f32[2,8,4,128]{3,2,0,1:T(4,128)S(1)} %get-tuple-element.109, f32[2,512,4]{2,0,1:T(2,128)} %bitcast.193, f32[2,64,4,128]{3,2,0,1:T(4,128)} %get-tuple-element.108, f32[2,512,4]{2,0,1:T(2,128)} %bitcast.194, ...), kind=kLoop, calls=%fused_computation.48 | loop fusion | flops 4718592 | bytes 3508224 | tf_op jit(solution)/shard_map/convert_element_type | solution.py:393
  100.8 0.8 all_to_all.29
  101.6 16.7 %all_to_all.35 = bf16[4,128,1024]{2,1,0:T(8,128)(2,1)S(1)} all-to-all(bf16[4,128,1024]{2,1,0:T(8,128)(2,1)S(1)} %all_to_all.29), channel_id=1, replica_groups=mesh['ctx'=128,'tensor'=4] {'tensor'}, dimensions={0} | all-to-all | bytes 2097152 | tf_op jit(solution)/shard_map/all_to_all | solution.py:395
  118.3 0.7 copy.69
  118.9 1.3 %copy.70 = bf16[128,4096]{1,0:T(8,128)(2,1)} copy(bf16[128,4096]{0,1:T(8,128)(2,1)S(1)} %bitcast.186) | data formatting | bytes 2097152 | tf_op jit(solution)/shard_map/all_to_all | solution.py:395
  (87 shorter events, 2.8 us)
Async XLA Ops:
  0.0 13.4 %copy-start.18 = (s32[2]{0:T(128)S(1)}, s32[2]{0:T(128)}, u32[]{:S(2)}) copy-start(s32[2]{0:T(128)} %param.12) | copy-start | bytes 28
  0.0 13.4 %copy-start.17 = (s32[2]{0:T(128)S(1)}, s32[2]{0:T(128)}, u32[]{:S(2)}) copy-start(s32[2]{0:T(128)} %param.13) | copy-start | bytes 28
  1.1 20.5 %copy-start = (bf16[128,4096]{1,0:T(8,128)(2,1)S(1)}, bf16[128,4096]{1,0:T(8,128)(2,1)}, u32[]{:S(2)}) copy-start(bf16[128,4096]{1,0:T(8,128)(2,1)} %q_ref.1) | copy-start | bytes 3145732
  1.9 18.3 %all-to-all-start = ((bf16[128,4,512]{2,0,1:T(8,128)(2,1)}), bf16[128,4,512]{2,0,1:T(8,128)(2,1)S(1)}, u32[]{:S(2)}, u32[]{:S(2)}) async-start(bf16[128,4,512]{2,0,1:T(8,128)(2,1)} %pad_maximum_fusion), calls=%async_computation | async-start | bytes 1048576 | tf_op jit(solution)/shard_map/all_to_all | solution.py:346
  14.2 6.6 %copy-start.15 = (pred[8,2]{0,1:T(4,128)(4,1)}, pred[8,2]{0,1:T(4,128)(4,1)S(1)}, u32[]{:S(2)}) copy-start(pred[8,2]{0,1:T(4,128)(4,1)S(1)} %iota_compare_fusion.5) | copy-start | bytes 52
  69.2 1.0 copy-start.1
  70.2 0.8 copy-start.3
  73.2 3.9 %copy-start.16 = (pred[8,2]{0,1:T(4,128)(4,1)S(1)}, pred[8,2]{0,1:T(4,128)(4,1)}, u32[]{:S(2)}) copy-start(pred[8,2]{0,1:T(4,128)(4,1)} %copy-done.15) | copy-start | bytes 52
  75.4 2.5 %copy-start.4 = (bf16[8,8,2,16,128]{4,3,2,1,0:T(8,128)(2,1)S(1)}, bf16[8,8,2,16,128]{4,3,2,1,0:T(8,128)(2,1)}, u32[]{:S(2)}) copy-start(bf16[8,8,2,16,128]{4,3,2,1,0:T(8,128)(2,1)} %copy-done.3) | copy-start | bytes 1572868
  78.2 1.2 %copy-start.2 = (bf16[2,8,64,512]{3,2,1,0:T(8,128)(2,1)S(1)}, bf16[2,8,64,512]{3,2,1,0:T(8,128)(2,1)}, u32[]{:S(2)}) copy-start(bf16[2,8,64,512]{3,2,1,0:T(8,128)(2,1)} %copy-done.1) | copy-start | bytes 3145732
  79.7 0.9 copy-start.9
  79.7 0.9 copy-start.11
  79.7 0.9 copy-start.12
  80.6 4.9 %copy-start.5 = (bf16[8,64,2,4,128]{4,3,2,1,0:T(4,128)(2,1)S(1)}, bf16[8,64,2,4,128]{4,3,2,1,0:T(4,128)(2,1)}, u32[]{:S(2)}) copy-start(bf16[8,64,2,4,128]{4,3,2,1,0:T(4,128)(2,1)} %reshape_reshape.15) | copy-start | bytes 3145732
  80.7 1.3 %copy-start.7 = (f32[2,64,4,128]{3,2,0,1:T(4,128)S(1)}, f32[2,64,4,128]{3,2,0,1:T(4,128)}, u32[]{:S(2)}) copy-start(f32[2,64,4,128]{3,2,0,1:T(4,128)} %get-tuple-element.345) | copy-start | bytes 786436 | tf_op jit(solution)/shard_map/while
  82.1 0.7 copy-start.8
  82.8 1.3 %copy-start.7 = (f32[2,64,4,128]{3,2,0,1:T(4,128)S(1)}, f32[2,64,4,128]{3,2,0,1:T(4,128)}, u32[]{:S(2)}) copy-start(f32[2,64,4,128]{3,2,0,1:T(4,128)} %get-tuple-element.345) | copy-start | bytes 786436 | tf_op jit(solution)/shard_map/while
  84.2 0.7 copy-start.8
  84.9 1.3 %copy-start.10 = (s32[8]{0:T(128)S(1)}, s32[8]{0:T(128)}, u32[]{:S(2)}) copy-start(s32[8]{0:T(128)} %iota_add_fusion) | copy-start | bytes 100
  84.9 1.3 %copy-start.13 = (f32[2,8,4]{1,2,0:T(4,128)S(1)}, f32[2,8,4]{1,2,0:T(4,128)}, u32[]{:S(2)}) copy-start(f32[2,8,4]{1,2,0:T(4,128)} %custom-call.4) | copy-start | bytes 772
  84.9 1.3 %copy-start.14 = (f32[2,8,4]{1,2,0:T(4,128)S(1)}, f32[2,8,4]{1,2,0:T(4,128)}, u32[]{:S(2)}) copy-start(f32[2,8,4]{1,2,0:T(4,128)} %custom-call.3) | copy-start | bytes 772
  87.9 4.6 %copy-start.6 = (f32[8,512,128]{2,1,0:T(8,128)S(1)}, f32[8,512,128]{2,1,0:T(8,128)}, u32[]{:S(2)}) copy-start(f32[8,512,128]{2,1,0:T(8,128)} %get-tuple-element.107) | copy-start | bytes 6291460

commit v3 on v2

--- a/solution.py
+++ b/solution.py
@@ -23,11 +23,13 @@
 
 
 def exchange_body(
-    q_ref, kv_ref, mid_ref, fk_ref, fv_ref,
-    q_out, prev_out, mid_out, fk_out, fv_out, near_out, max_out, sum_out,
+    q_ref, kv_ref, mid_ref, fk_ref, fv_ref, mid_off, far_off,
+    result,
+    q_out, prev_out, mid_out, fk_out, fv_out, near_out, max_out, sum_out, staged,
     local_sem, prev_send, prev_recv, q_send, q_recv, x_send, x_recv,
     mid_send, mid_recv, fwd_send, fwd_recv,
     k1_send, k1_recv, v1_send, v1_recv, k2_send, k2_recv, v2_send, v2_recv,
+    back_send, back_recv,
 ):
     place = lax.axis_index("ctx")
     lane = lax.axis_index("tensor")
@@ -242,11 +244,132 @@
     near(1)
     ahead[0].wait_recv()
     near(0)
+    own_mid.wait()
+    for copy in forwards:
+        copy.wait_recv()
+    tokens = kv_ref.shape[0]
+    group = per_group * HEAD_DIM
+
+    def picked(head, offset, rate):
+        count = tokens // rate
+        row = lax.broadcasted_iota(jnp.int32, (count, tokens), 0)
+        col = lax.broadcasted_iota(jnp.int32, (count, tokens), 1)
+        chosen = jnp.where(col == row * rate + offset, 1.0, 0.0).astype(jnp.bfloat16)
+        wide = q_out[:, :, head * group : (head + 1) * group].reshape(tokens, group)
+        rows = jnp.dot(chosen, wide, preferred_element_type=jnp.float32)
+        parts = [rows[:, g * HEAD_DIM : (g + 1) * HEAD_DIM] for g in range(per_group)]
+        return jnp.concatenate(parts, 0).astype(jnp.bfloat16)
+
+    def attend(rows, key_rows, value_rows, bias):
+        scores = lax.dot_general(
+            rows, key_rows, (((1,), (1,)), ((), ())), preferred_element_type=jnp.float32
+        )
+        scores = scores * HEAD_DIM ** (-0.5) + jnp.concatenate([bias] * per_group, 0)
+        maxima = jnp.max(scores, axis=1, keepdims=True)
+        powers = jnp.exp(scores - maxima)
+        totals = jnp.sum(powers, axis=1, keepdims=True)
+        weighted = jnp.dot(
+            powers.astype(jnp.bfloat16), value_rows, preferred_element_type=jnp.float32
+        )
+        return maxima, totals, weighted
+
+    def mid_stats(head):
+        count = tokens // RATE_MID
+        span = 2 * RING * count
+        row = lax.broadcasted_iota(jnp.int32, (count, span), 0)
+        col = lax.broadcasted_iota(jnp.int32, (count, span), 1)
+        bias = jnp.where(col <= lax.rem(place, 2 * RING) * count + row, 0.0, NEG_FILL)
+        first = head * HEAD_DIM
+        second = (kv_local + head) * HEAD_DIM
+        return attend(
+            picked(head, mid_off[head], RATE_MID),
+            mid_out[:, :, :, first : first + HEAD_DIM].reshape(span, HEAD_DIM),
+            mid_out[:, :, :, second : second + HEAD_DIM].reshape(span, HEAD_DIM),
+            bias,
+        )
+
+    mids = [mid_stats(head) for head in range(kv_local)]
     k_ring.landed(4)
     v_ring.landed(4)
-    for copy in forwards:
-        copy.wait_recv()
-    own_mid.wait()
+
+    def far_stats(head):
+        count = tokens // RATE_FAR
+        span = total * kv_local * count
+        row = lax.broadcasted_iota(jnp.int32, (count, span), 0)
+        col = lax.broadcasted_iota(jnp.int32, (count, span), 1)
+        inner = lax.rem(col, count)
+        owner = lax.rem(col // count, kv_local)
+        block = col // (count * kv_local)
+        source = lax.rem(block, 2) * (RING * RING) + block // 2
+        allowed = (owner == head) & (source * count + inner <= place * count + row)
+        key_rows = fk_out[...].reshape(span, HEAD_DIM)
+        value_rows = jnp.concatenate(
+            [fv_out[:, i].reshape(span // RING, HEAD_DIM) for i in range(RING)], 0
+        )
+        return attend(
+            picked(head, far_off[head], RATE_FAR),
+            key_rows, value_rows, jnp.where(allowed, 0.0, NEG_FILL),
+        )
+
+    fars = [far_stats(head) for head in range(kv_local)]
+    token = lax.broadcasted_iota(jnp.int32, (tokens, HEAD_DIM), 0)
+
+    def spread(stats, head, g, offset, rate):
+        count = tokens // rate
+        full = []
+        for part in stats:
+            part = jnp.broadcast_to(part[g * count : (g + 1) * count], (count, HEAD_DIM))
+            part = jnp.broadcast_to(part[:, None, :], (count, rate, HEAD_DIM))
+            full.append(part.reshape(tokens, HEAD_DIM))
+        full[0] = jnp.where(lax.rem(token, rate) == offset, full[0], NEG_FILL)
+        return full
+
+    def send_back(head):
+        for step in range(1, lanes):
+            other = lax.rem(lane + step, lanes)
+            start = pl.multiple_of(lane * width + head * group, group)
+            backs.append(
+                remote(
+                    staged.at[other, :, pl.ds(head * group, group)],
+                    result.at[:, pl.ds(start, group)],
+                    back_send.at[head, step], back_recv.at[head, step], {"tensor": other},
+                )
+            )
+
+    backs = []
+    for head in range(kv_local):
+        for g in range(per_group):
+            index = head * per_group + g
+            near_parts = (
+                jnp.broadcast_to(max_out[index], (tokens, HEAD_DIM)),
+                jnp.broadcast_to(sum_out[index], (tokens, HEAD_DIM)),
+                near_out[index],
+            )
+            branches = (
+                near_parts,
+                spread(mids[head], head, g, mid_off[head], RATE_MID),
+                spread(fars[head], head, g, far_off[head], RATE_FAR),
+            )
+            highest = jnp.maximum(
+                jnp.maximum(branches[0][0], branches[1][0]), branches[2][0]
+            )
+            numerator = jnp.zeros((tokens, HEAD_DIM), jnp.float32)
+            denominator = jnp.zeros((tokens, HEAD_DIM), jnp.float32)
+            for maxima, totals, weighted in branches:
+                factor = jnp.exp(maxima - highest)
+                denominator = denominator + factor * totals
+                numerator = numerator + factor * weighted
+            attended = (numerator / denominator).astype(jnp.bfloat16)
+            staged[:, :, index * HEAD_DIM : (index + 1) * HEAD_DIM] = attended.reshape(
+                lanes, tokens // lanes, HEAD_DIM
+            )
+            if head > 0 and g == 0:
+                send_back(head - 1)
+    send_back(kv_local - 1)
+    own_back = pltpu.make_async_copy(
+        staged.at[lane], result.at[:, columns(lane)], local_sem.at[4]
+    )
+    own_back.start()
     x_k.wait_send()
     x_v.wait_send()
     for step in order:
@@ -256,60 +379,43 @@
         copy.wait_send()
     for ring in (mid_ring, k_ring, v_ring):
         ring.finish()
-
-
-def exchange(queries, kv_rows, mid_kv, far_k, far_v):
+    own_back.wait()
+    for copy in backs:
+        copy.wait()
+
+
+def exchange(queries, kv_rows, mid_kv, far_k, far_v, mid_offsets, far_offsets):
     lanes = lax.axis_size("tensor")
     own, wide = queries.shape
     rows = kv_rows.shape[0]
     heads = HEADS // lanes
-    sizes = [4, 4, 4, 4, 4, 2, 2] + [2 * RING] * 12
-    stat = jax.ShapeDtypeStruct((heads, rows, 1), jnp.float32)
+    kv_local = mid_offsets.shape[0]
+    sizes = [5, 4, 4, 4, 4, 2, 2] + [2 * RING] * 12
+    vmem = pl.BlockSpec(memory_space=pltpu.VMEM)
+    smem = pl.BlockSpec(memory_space=pltpu.SMEM)
     return pl.pallas_call(
         exchange_body,
-        out_shape=[
-            jax.ShapeDtypeStruct((lanes, own, wide // lanes), jnp.bfloat16),
-            jax.ShapeDtypeStruct(kv_rows.shape, jnp.bfloat16),
-            jax.ShapeDtypeStruct((2, RING) + mid_kv.shape, jnp.bfloat16),
-            jax.ShapeDtypeStruct((RING, RING, 2) + far_k.shape, jnp.bfloat16),
-            jax.ShapeDtypeStruct((RING, RING, 2) + far_v.shape, jnp.bfloat16),
-            jax.ShapeDtypeStruct((heads, rows, HEAD_DIM), jnp.float32),
-            stat,
-            stat,
-        ],
-        in_specs=[pl.BlockSpec(memory_space=pltpu.VMEM)] * 5,
-        out_specs=[pl.BlockSpec(memory_space=pltpu.VMEM)] * 8,
-        scratch_shapes=[pltpu.SemaphoreType.DMA((size,)) for size in sizes],
+        out_shape=jax.ShapeDtypeStruct((own, wide), jnp.bfloat16),
+        in_specs=[vmem] * 5 + [smem] * 2,
+        out_specs=vmem,
+        scratch_shapes=[
+            pltpu.VMEM((lanes, own, wide // lanes), jnp.bfloat16),
+            pltpu.VMEM(kv_rows.shape, jnp.bfloat16),
+            pltpu.VMEM((2, RING) + mid_kv.shape, jnp.bfloat16),
+            pltpu.VMEM((RING, RING, 2) + far_k.shape, jnp.bfloat16),
+            pltpu.VMEM((RING, RING, 2) + far_v.shape, jnp.bfloat16),
+            pltpu.VMEM((heads, rows, HEAD_DIM), jnp.float32),
+            pltpu.VMEM((heads, rows, 1), jnp.float32),
+            pltpu.VMEM((heads, rows, 1), jnp.float32),
+            pltpu.VMEM((lanes, own, wide // lanes), jnp.bfloat16),
+        ]
+        + [pltpu.SemaphoreType.DMA((size,)) for size in sizes]
+        + [pltpu.SemaphoreType.DMA((kv_local, lanes))] * 2,
         compiler_params=pltpu.CompilerParams(
-            collective_id=0, has_side_effects=True, vmem_limit_bytes=48 * 2**20
+            collective_id=0, has_side_effects=True, vmem_limit_bytes=56 * 2**20
         ),
         name="exchange",
-    )(queries, kv_rows, mid_kv, far_k, far_v)
-
-
-def head_stats(query_rows, key_rows, value_rows, allowed, scale_factor):
-    scores = (
-        jnp.einsum("agd,bd->agb", query_rows, key_rows, preferred_element_type=jnp.float32)
-        * scale_factor
-    )
-    scores = jnp.where(allowed[:, None, :], scores, NEG_FILL)
-    maxima = jnp.max(scores, axis=-1)
-    powers = jnp.exp(scores - maxima[..., None])
-    totals = jnp.sum(powers, axis=-1)
-    weights = powers.astype(jnp.bfloat16)
-    weighted = jnp.einsum("agb,bd->agd", weights, value_rows, preferred_element_type=jnp.float32)
-    return (maxima, totals, weighted)
-
-
-def branch_stats(query_rows, kv_rows, allowed, scale_factor):
-    query_heads = query_rows.transpose(1, 0, 2, 3)
-    key_heads = kv_rows[:, 0].transpose(1, 0, 2)
-    value_heads = kv_rows[:, 1].transpose(1, 0, 2)
-
-    def one_head(items):
-        return head_stats(items[0], items[1], items[2], allowed, scale_factor)
-
-    return lax.map(one_head, (query_heads, key_heads, value_heads))
+    )(queries, kv_rows, mid_kv, far_k, far_v, mid_offsets, far_offsets)
 
 
 def pick_rows(rows, offsets, rate, kv_dim):
@@ -320,21 +426,6 @@
     hit_shape[kv_dim + 1] = offsets.shape[0]
     kept = jnp.where(chosen.reshape(hit_shape), shaped, jnp.zeros((), rows.dtype))
     return jnp.sum(kept, axis=1)
-
-
-def spread_stats(stats, offsets, rate):
-    maxima, totals, weighted = stats
-    kv_local = maxima.shape[0]
-    per_group = maxima.shape[2]
-    chosen = jnp.arange(rate, dtype=jnp.int32)[None, :] == offsets[:, None]
-    maxima = jnp.where(chosen[:, None, :, None], maxima[:, :, None, :], NEG_FILL).reshape(
-        kv_local, -1, per_group
-    )
-    totals = jnp.where(chosen[:, None, :, None], totals[:, :, None, :], jnp.float32(0.0)).reshape(
-        kv_local, -1, per_group
-    )
-    weighted = jnp.where(chosen[:, None, :, None, None], weighted[:, :, None], jnp.float32(0.0))
-    return (maxima, totals, weighted.reshape(kv_local, -1, per_group, weighted.shape[-1]))
 
 
 def on_device(queries, keys, values, mid_offsets, far_offsets):
@@ -346,11 +437,6 @@
     kv_rows = lax.all_to_all(kv_rows, "tensor", split_axis=1, concat_axis=0, tiled=True)
     tok_rows = kv_rows.shape[0]
     kv_local = mid_offsets.shape[0]
-    per_group = HEADS // KV_HEADS
-    scale_factor = HEAD_DIM ** (-0.5)
-    ctx_count = lax.axis_size("ctx")
-    ctx_place = lax.axis_index("ctx")
-    team_size = min(16, ctx_count)
     kv_dims = (2, kv_local, HEAD_DIM)
     kv_heads = kv_rows.reshape((tok_rows,) + kv_dims)
     mid_kv = pick_rows(kv_heads, mid_offsets, RATE_MID, 2)
@@ -358,41 +444,10 @@
     mid_count = tok_rows // RATE_MID
     far_count = tok_rows // RATE_FAR
     far_flat = far_kv.transpose(1, 2, 0, 3).reshape(2, kv_local * far_count, HEAD_DIM)
-    gathered, _, mid_all, far_k, far_v, *near = exchange(
-        queries, kv_rows, mid_kv.reshape(mid_count, -1), far_flat[0], far_flat[1]
+    return exchange(
+        queries, kv_rows, mid_kv.reshape(mid_count, -1), far_flat[0], far_flat[1],
+        mid_offsets, far_offsets,
     )
-    mid_all = mid_all.reshape((team_size * mid_count,) + kv_dims)
-    far_split = (RING, RING, 2, kv_local, far_count, HEAD_DIM)
-    far_k = far_k.reshape(far_split).transpose(3, 2, 0, 1, 4, 5)
-    far_v = far_v.reshape(far_split).transpose(3, 2, 1, 0, 4, 5)
-    far_all = jnp.stack(
-        [far_k.reshape(kv_local, -1, HEAD_DIM), far_v.reshape(kv_local, -1, HEAD_DIM)]
-    ).transpose(2, 0, 1, 3)
-    query_rows = gathered.reshape(tok_rows, kv_local, per_group, HEAD_DIM)
-    near = [part.reshape(kv_local, per_group, tok_rows, -1).transpose(0, 2, 1, 3) for part in near]
-    near_stats = (near[1][..., 0], near[2][..., 0], near[0])
-    mid_queries = pick_rows(query_rows, mid_offsets, RATE_MID, 1)
-    far_queries = pick_rows(query_rows, far_offsets, RATE_FAR, 1)
-    mid_position = ctx_place % team_size * mid_count + jnp.arange(mid_count)[:, None]
-    mid_allowed = jnp.arange(team_size * mid_count)[None, :] <= mid_position
-    mid_stats = spread_stats(
-        branch_stats(mid_queries, mid_all, mid_allowed, scale_factor), mid_offsets, RATE_MID
-    )
-    far_position = ctx_place * far_count + jnp.arange(far_count)[:, None]
-    far_allowed = jnp.arange(ctx_count * far_count)[None, :] <= far_position
-    far_stats = spread_stats(
-        branch_stats(far_queries, far_all, far_allowed, scale_factor), far_offsets, RATE_FAR
-    )
-    highest = jnp.maximum(jnp.maximum(near_stats[0], mid_stats[0]), far_stats[0])
-    denominator = jnp.zeros_like(highest)
-    numerator = jnp.zeros(near_stats[2].shape, jnp.float32)
-    for stats in (near_stats, mid_stats, far_stats):
-        factor = jnp.exp(stats[0] - highest)
-        denominator = denominator + factor * stats[1]
-        numerator = numerator + factor[..., None] * stats[2]
-    attended = (numerator / denominator[..., None]).astype(jnp.bfloat16)
-    attended = attended.transpose(1, 0, 2, 3).reshape(tok_rows, kv_local * per_group * HEAD_DIM)
-    return lax.all_to_all(attended, "tensor", split_axis=0, concat_axis=1, tiled=True)
 
 
 def solution(mesh):

time: 121 us -> 90 us (0.74)
  other arithmetic: 19.1 us -> 2.09 us
  blocking collectives: 16.7 us -> 0 us
  Pallas kernels: 47.5 us -> 64 us
  local copies, waits for them, and re-layouts: 17.4 us -> 5.92 us
  matrix products: 2.54 us -> 0 us
  waiting for transfers between devices: 6.02 us -> 7.31 us
    all_to_all x1 -> x0, blocking collectives: 16.7 us -> none  [on_device(): lax.all_to_all(attended, 'tensor', split_axis=0, concat_axis=1, tiled=True)]
    pallas_call x1, Pallas kernels: 47.5 us -> 64 us  [exchange(): pl.pallas_call(exchange_body, out_shape=jax.ShapeDtypeStruct((own, wide),...]
    convert_element_type x1 -> x0, other arithmetic: 8.33 us -> none  [on_device(): attended = (numerator / denominator[..., None]).astype(jnp.bfloat16)]
    pallas_call x2 -> x0, other arithmetic: 4.4 us -> none  [exchange(): pl.pallas_call(exchange_body, out_shape=[jax.ShapeDtypeStruct((lanes, own...]
    mul x3 -> x0, local copies, waits for them, and re-layouts: 3.09 us -> none  [on_device(): numerator = numerator + factor[..., None] * stats[2]]
    all_to_all x3 -> x0, local copies, waits for them, and re-layouts: 2.73 us -> none  [on_device(): lax.all_to_all(attended, 'tensor', split_axis=0, concat_axis=1, tiled=True)]
    dot_general x8 -> x0, matrix products: 2.54 us -> none  [the longest x4 1.37 us: head_stats(): jnp.einsum('agd,bd->agb', query_rows, key_rows, preferred_element_type=jn...]
    another operation x2 -> x1, local copies, waits for them, and re-layouts: 1.69 us -> 0.12 us  [pick_rows(): shaped = rows.reshape((rows.shape[0] // rate, rate) + rows.shape[1:])]
  transfers between devices with their start and end apart: 1 -> 1, of which waited for: 1 -> 1; matrix products, arithmetic and copies ran while one was open for 2% -> 0% of each run, Pallas kernels for 0% -> 0%
where the time goes in v3:
time: 90 us; the launch traced here: 89.8 us
  Pallas kernels  64 us (71%)
  starting transfers between devices  10.4 us (12%)
  waiting for transfers between devices  7.31 us (8%)
  local copies, waits for them, and re-layouts  5.92 us (7%)
  other arithmetic  2.09 us (2%)
    pallas_call x1, Pallas kernels, exchange(): pl.pallas_call(exchange_body, out_shape=jax.ShapeDtypeStruct((own, wide),...  64 us
    all_to_all x1, starting transfers between devices, on_device(): lax.all_to_all(kv_rows, 'tensor', split_axis=1, concat_axis=0, tiled=True)  10.4 us
    all_to_all x1, waiting for transfers between devices, on_device(): lax.all_to_all(kv_rows, 'tensor', split_axis=1, concat_axis=0, tiled=True)  7.31 us
    unnamed x7, local copies, waits for them, and re-layouts  2.88 us
  transfers between devices with their start and end apart: 1, of which 1 were waited for; matrix products, arithmetic and copies ran while one was open for 0% of the time, Pallas kernels for 0%

profile of v3, /device:TPU:1, one launch (start us, length us, event | category | flops | bytes accessed | tf_op | source)
XLA Modules:
  0.0 89.8 jit_solution(413609074736402999)
XLA Ops:
  0.0 1.1 %copy_bitcast_fusion = (bf16[128,4,256]{2,0,1:T(8,128)(2,1)S(1)}, bf16[128,4,256]{2,0,1:T(8,128)(2,1)S(1)}) fusion(bf16[16,4,8,256]{3,2,1,0:T(8,128)(2,1)} %bitcast.21, bf16[16,4,8,256]{3,2,1,0:T(8,128)(2,1)} %bitcast.22), kind=kLoop, calls=%fused_computation.4 | loop fusion | bytes 1048576 | tf_op jit(solution)/shard_map/reshape | solution.py:435
  1.1 0.8 pad_maximum_fusion
  1.9 0.0 copy-start.2
  1.9 10.4 %all-to-all-start = ((bf16[128,4,512]{2,0,1:T(8,128)(2,1)}), bf16[128,4,512]{2,0,1:T(8,128)(2,1)S(1)}, u32[]{:S(2)}, u32[]{:S(2)}) async-start(bf16[128,4,512]{2,0,1:T(8,128)(2,1)} %pad_maximum_fusion), calls=%async_computation | async-start | bytes 1048576 | tf_op jit(solution)/shard_map/all_to_all | solution.py:437
  12.4 0.0 copy-done.2
  12.4 0.0 copy-start.1
  12.4 0.1 iota_compare_fusion.1
  12.4 0.6 copy-done.1
  13.0 7.3 %all-to-all-done = bf16[128,4,512]{2,0,1:T(8,128)(2,1)S(1)} async-done(((bf16[128,4,512]{2,0,1:T(8,128)(2,1)}), bf16[128,4,512]{2,0,1:T(8,128)(2,1)S(1)}, u32[]{:S(2)}, u32[]{:S(2)}) %all-to-all-start) | async-done | bytes 524320 | tf_op jit(solution)/shard_map/all_to_all | solution.py:437
  20.3 0.0 copy-start
  20.3 0.5 select_reduce_fusion
  20.9 0.7 reshape.67.mid_ref
  21.5 0.1 reshape_reshape.7
  21.7 0.0 copy-done
  21.7 0.6 fusion
  22.3 0.6 copy.18
  22.9 0.6 copy.19
  23.5 64.0 %exchange.1 = bf16[128,4096]{1,0:T(8,128)(2,1)} custom-call(bf16[128,4096]{1,0:T(8,128)(2,1)} %q_ref.1, bf16[512,512]{1,0:T(8,128)(2,1)} %bitcast.20, bf16[64,512]{1,0:T(8,128)(2,1)} %reshape.67.mid_ref, bf16[16,128]{1,0:T(8,128)(2,1)} %bitcast.25, bf16[16,128]{1,0:T(8,128)(2,1)} %bitcast.24, s32[2]{0:T(128)} %mid_off.1, s32[2]{0:T(128)} %far_off.1), custom_call_target="tpu_custom_call" | custom-call | tf_op jit(solution)/shard_map/exchange/pallas_call | solution.py:396
  87.5 2.3 %copy.21 = bf16[128,4096]{1,0:T(8,128)(2,1)} copy(bf16[128,4096]{1,0:T(8,128)(2,1)} %exchange.1) | data formatting | bytes 2097152
  (2 shorter events, 0.0 us)
Async XLA Ops:
  1.9 10.5 %copy-start.2 = (s32[2]{0:T(128)S(1)}, s32[2]{0:T(128)}, u32[]{:S(2)}) copy-start(s32[2]{0:T(128)} %mid_off.1) | copy-start | bytes 28
  1.9 18.4 %all-to-all-start = ((bf16[128,4,512]{2,0,1:T(8,128)(2,1)}), bf16[128,4,512]{2,0,1:T(8,128)(2,1)S(1)}, u32[]{:S(2)}, u32[]{:S(2)}) async-start(bf16[128,4,512]{2,0,1:T(8,128)(2,1)} %pad_maximum_fusion), calls=%async_computation | async-start | bytes 1048576 | tf_op jit(solution)/shard_map/all_to_all | solution.py:437
  12.4 0.7 copy-start.1
  20.3 1.3 %copy-start = (bf16[128,4,512]{2,0,1:T(8,128)(2,1)}, bf16[128,4,512]{2,0,1:T(8,128)(2,1)S(1)}, u32[]{:S(2)}) copy-start(bf16[128,4,512]{2,0,1:T(8,128)(2,1)S(1)} %all-to-all-done) | copy-start | bytes 1572868

commit v4 on v3

--- a/solution.py
+++ b/solution.py
@@ -23,13 +23,14 @@
 
 
 def exchange_body(
-    q_ref, kv_ref, mid_ref, fk_ref, fv_ref, mid_off, far_off,
+    q_ref, key_ref, value_ref, mid_off, far_off,
     result,
+    kv_ref, mid_ref, fk_ref, fv_ref,
     q_out, prev_out, mid_out, fk_out, fv_out, near_out, max_out, sum_out, staged,
     local_sem, prev_send, prev_recv, q_send, q_recv, x_send, x_recv,
     mid_send, mid_recv, fwd_send, fwd_recv,
     k1_send, k1_recv, v1_send, v1_recv, k2_send, k2_recv, v2_send, v2_recv,
-    back_send, back_recv,
+    back_send, back_recv, kv_send, kv_recv,
 ):
     place = lax.axis_index("ctx")
     lane = lax.axis_index("tensor")
@@ -111,14 +112,71 @@
             for copy in self.sent.values():
                 copy.wait_send()
 
-    own_k = pltpu.make_async_copy(fk_ref, fk_out.at[y, z, x], local_sem.at[0])
-    own_v = pltpu.make_async_copy(fv_ref, fv_out.at[z, y, x], local_sem.at[1])
+    tokens, kv_wide = kv_ref.shape
+    half = kv_wide // 2
+    mine_rows = pl.ds(pl.multiple_of(lane * CHUNK, CHUNK), CHUNK)
+
+    def kv_columns(index):
+        return pl.ds(pl.multiple_of(index * half, half), half)
+
+    shares = []
+    for part, source in enumerate((key_ref, value_ref)):
+        target = kv_ref.at[mine_rows, pl.ds(part * half, half)]
+        own_part = pltpu.make_async_copy(
+            source.at[:, kv_columns(lane)], target, local_sem.at[5 + part]
+        )
+        own_part.start()
+        shares.append((own_part, target))
+    arriving = []
+    for step in (2, 1, 3):
+        other = lax.rem(lane + step, lanes)
+        for part, source in enumerate((key_ref, value_ref)):
+            arriving.append(
+                remote(
+                    source.at[:, kv_columns(other)], shares[part][1],
+                    kv_send.at[part, step], kv_recv.at[part, step], {"tensor": other},
+                )
+            )
+    own_q = pltpu.make_async_copy(q_ref.at[:, columns(lane)], q_out.at[lane], local_sem.at[3])
+    own_q.start()
+    moves = []
+    for step in range(1, lanes):
+        other = lax.rem(lane + step, lanes)
+        moves.append(
+            remote(
+                q_ref.at[:, columns(other)], q_out.at[lane],
+                q_send.at[step], q_recv.at[step], {"tensor": other},
+            )
+        )
+    for own_part, _ in shares:
+        own_part.wait()
+    for copy in arriving:
+        copy.wait_recv()
+
+    def one_hot(offset, rate):
+        count = tokens // rate
+        row = lax.broadcasted_iota(jnp.int32, (count, tokens), 0)
+        col = lax.broadcasted_iota(jnp.int32, (count, tokens), 1)
+        return jnp.where(col == row * rate + offset, 1.0, 0.0).astype(jnp.bfloat16)
+
+    mid_hot = [one_hot(mid_off[head], RATE_MID) for head in range(kv_local)]
+    far_hot = [one_hot(far_off[head], RATE_FAR) for head in range(kv_local)]
+    far_rows = []
+    for part in range(2):
+        for head in range(kv_local):
+            cols = slice((part * kv_local + head) * HEAD_DIM, (part * kv_local + head + 1) * HEAD_DIM)
+            block = kv_ref[:, cols]
+            mid_ref[:, cols] = jnp.dot(
+                mid_hot[head], block, preferred_element_type=jnp.float32
+            ).astype(jnp.bfloat16)
+            far_rows.append(
+                jnp.dot(far_hot[head], block, preferred_element_type=jnp.float32)
+            )
+    fk_ref[...] = jnp.concatenate(far_rows[:kv_local], 0).astype(jnp.bfloat16)
+    fv_ref[...] = jnp.concatenate(far_rows[kv_local:], 0).astype(jnp.bfloat16)
+
     own_mid = pltpu.make_async_copy(mid_ref, mid_out.at[parity, z], local_sem.at[2])
-    own_q = pltpu.make_async_copy(q_ref.at[:, columns(lane)], q_out.at[lane], local_sem.at[3])
-    for copy in (own_k, own_v, own_mid, own_q):
-        copy.start()
-    x_k = remote(fk_ref, fk_out.at[y, z, x], x_send.at[0], x_recv.at[0], x_peer)
-    x_v = remote(fv_ref, fv_out.at[z, y, x], x_send.at[1], x_recv.at[1], x_peer)
+    own_mid.start()
     mid_ring = Ring(
         lambda i: mid_out.at[parity, i], z, z_peer, mid_send, mid_recv, mid_ref, (3, 4)
     )
@@ -126,23 +184,22 @@
     forwards = [
         remote(mid_ref, mid_out.at[parity, z], fwd_send.at[0], fwd_recv.at[0], y_pair)
     ]
-    moves = []
-    for step in range(1, lanes):
-        other = lax.rem(lane + step, lanes)
-        moves.append(
-            remote(
-                q_ref.at[:, columns(other)], q_out.at[lane],
-                q_send.at[step], q_recv.at[step], {"tensor": other},
-            )
-        )
-    chunks = kv_ref.shape[0] // CHUNK
+    own_k = pltpu.make_async_copy(fk_ref, fk_out.at[y, z, x], local_sem.at[0])
+    own_v = pltpu.make_async_copy(fv_ref, fv_out.at[z, y, x], local_sem.at[1])
+    own_k.start()
+    own_v.start()
+    x_k = remote(fk_ref, fk_out.at[y, z, x], x_send.at[0], x_recv.at[0], x_peer)
+    x_v = remote(fv_ref, fv_out.at[z, y, x], x_send.at[1], x_recv.at[1], x_peer)
     ahead = {}
-    for chunk in reversed(range(chunks)):
+
+    def pass_on(chunk):
         rows = pl.ds(chunk * CHUNK, CHUNK)
         ahead[chunk] = remote(
             kv_ref.at[rows], prev_out.at[rows], prev_send.at[chunk], prev_recv.at[chunk], after
         )
+
     order = [4, 3, 5, 2, 6, 1, 7]
+    pass_on(3)
     own_k.wait()
     own_v.wait()
     x_k.wait_recv()
@@ -169,6 +226,7 @@
             mid_ring.start(step)
 
     mid_step(2)
+    pass_on(2)
     for step in order:
         firsts_k[step].wait_recv()
         firsts_v[step].wait_recv()
@@ -219,14 +277,16 @@
                 sum_out[head * per_group + g, first : first + CHUNK] = totals[mine]
 
     mid_step(3)
+    pass_on(1)
+    own_q.wait()
+    for copy in moves:
+        copy.wait_recv()
     k_ring.landed(1)
     k_ring.start(2)
     v_ring.landed(1)
     v_ring.start(2)
-    own_q.wait()
+    pass_on(0)
     ahead[3].wait_recv()
-    for copy in moves:
-        copy.wait_recv()
     near(3)
     mid_step(4)
     k_ring.landed(2)
@@ -247,14 +307,9 @@
     own_mid.wait()
     for copy in forwards:
         copy.wait_recv()
-    tokens = kv_ref.shape[0]
     group = per_group * HEAD_DIM
 
-    def picked(head, offset, rate):
-        count = tokens // rate
-        row = lax.broadcasted_iota(jnp.int32, (count, tokens), 0)
-        col = lax.broadcasted_iota(jnp.int32, (count, tokens), 1)
-        chosen = jnp.where(col == row * rate + offset, 1.0, 0.0).astype(jnp.bfloat16)
+    def picked(head, chosen):
         wide = q_out[:, :, head * group : (head + 1) * group].reshape(tokens, group)
         rows = jnp.dot(chosen, wide, preferred_element_type=jnp.float32)
         parts = [rows[:, g * HEAD_DIM : (g + 1) * HEAD_DIM] for g in range(per_group)]
@@ -282,7 +337,7 @@
         first = head * HEAD_DIM
         second = (kv_local + head) * HEAD_DIM
         return attend(
-            picked(head, mid_off[head], RATE_MID),
+            picked(head, mid_hot[head]),
             mid_out[:, :, :, first : first + HEAD_DIM].reshape(span, HEAD_DIM),
             mid_out[:, :, :, second : second + HEAD_DIM].reshape(span, HEAD_DIM),
             bias,
@@ -307,7 +362,7 @@
             [fv_out[:, i].reshape(span // RING, HEAD_DIM) for i in range(RING)], 0
         )
         return attend(
-            picked(head, far_off[head], RATE_FAR),
+            picked(head, far_hot[head]),
             key_rows, value_rows, jnp.where(allowed, 0.0, NEG_FILL),
         )
 
@@ -375,7 +430,7 @@
     for step in order:
         firsts_k[step].wait_send()
         firsts_v[step].wait_send()
-    for copy in forwards + moves + list(ahead.values()):
+    for copy in arriving + forwards + moves + list(ahead.values()):
         copy.wait_send()
     for ring in (mid_ring, k_ring, v_ring):
         ring.finish()
@@ -384,70 +439,46 @@
         copy.wait()
 
 
-def exchange(queries, kv_rows, mid_kv, far_k, far_v, mid_offsets, far_offsets):
+def exchange(queries, keys, values, mid_offsets, far_offsets):
     lanes = lax.axis_size("tensor")
     own, wide = queries.shape
-    rows = kv_rows.shape[0]
+    rows = own * lanes
     heads = HEADS // lanes
     kv_local = mid_offsets.shape[0]
-    sizes = [5, 4, 4, 4, 4, 2, 2] + [2 * RING] * 12
+    kv_shape = (rows, 2 * kv_local * HEAD_DIM)
+    mid_shape = (rows // RATE_MID, kv_shape[1])
+    far_shape = (kv_local * rows // RATE_FAR, HEAD_DIM)
+    sizes = [7, 4, 4, 4, 4, 2, 2] + [2 * RING] * 12
     vmem = pl.BlockSpec(memory_space=pltpu.VMEM)
     smem = pl.BlockSpec(memory_space=pltpu.SMEM)
     return pl.pallas_call(
         exchange_body,
         out_shape=jax.ShapeDtypeStruct((own, wide), jnp.bfloat16),
-        in_specs=[vmem] * 5 + [smem] * 2,
+        in_specs=[vmem] * 3 + [smem] * 2,
         out_specs=vmem,
         scratch_shapes=[
+            pltpu.VMEM(kv_shape, jnp.bfloat16),
+            pltpu.VMEM(mid_shape, jnp.bfloat16),
+            pltpu.VMEM(far_shape, jnp.bfloat16),
+            pltpu.VMEM(far_shape, jnp.bfloat16),
             pltpu.VMEM((lanes, own, wide // lanes), jnp.bfloat16),
-            pltpu.VMEM(kv_rows.shape, jnp.bfloat16),
-            pltpu.VMEM((2, RING) + mid_kv.shape, jnp.bfloat16),
-            pltpu.VMEM((RING, RING, 2) + far_k.shape, jnp.bfloat16),
-            pltpu.VMEM((RING, RING, 2) + far_v.shape, jnp.bfloat16),
+            pltpu.VMEM(kv_shape, jnp.bfloat16),
+            pltpu.VMEM((2, RING) + mid_shape, jnp.bfloat16),
+            pltpu.VMEM((RING, RING, 2) + far_shape, jnp.bfloat16),
+            pltpu.VMEM((RING, RING, 2) + far_shape, jnp.bfloat16),
             pltpu.VMEM((heads, rows, HEAD_DIM), jnp.float32),
             pltpu.VMEM((heads, rows, 1), jnp.float32),
             pltpu.VMEM((heads, rows, 1), jnp.float32),
             pltpu.VMEM((lanes, own, wide // lanes), jnp.bfloat16),
         ]
         + [pltpu.SemaphoreType.DMA((size,)) for size in sizes]
-        + [pltpu.SemaphoreType.DMA((kv_local, lanes))] * 2,
+        + [pltpu.SemaphoreType.DMA((kv_local, lanes))] * 2
+        + [pltpu.SemaphoreType.DMA((2, lanes))] * 2,
         compiler_params=pltpu.CompilerParams(
             collective_id=0, has_side_effects=True, vmem_limit_bytes=56 * 2**20
         ),
         name="exchange",
-    )(queries, kv_rows, mid_kv, far_k, far_v, mid_offsets, far_offsets)
-
-
-def pick_rows(rows, offsets, rate, kv_dim):
-    shaped = rows.reshape((rows.shape[0] // rate, rate) + rows.shape[1:])
-    chosen = jnp.arange(rate, dtype=jnp.int32)[:, None] == offsets[None, :]
-    hit_shape = [1] * shaped.ndim
-    hit_shape[1] = rate
-    hit_shape[kv_dim + 1] = offsets.shape[0]
-    kept = jnp.where(chosen.reshape(hit_shape), shaped, jnp.zeros((), rows.dtype))
-    return jnp.sum(kept, axis=1)
-
-
-def on_device(queries, keys, values, mid_offsets, far_offsets):
-    count = lax.axis_size("tensor")
-    own = queries.shape[0]
-    kv_rows = jnp.concatenate(
-        [keys.reshape(own, count, -1), values.reshape(own, count, -1)], axis=2
-    ).reshape(own, -1)
-    kv_rows = lax.all_to_all(kv_rows, "tensor", split_axis=1, concat_axis=0, tiled=True)
-    tok_rows = kv_rows.shape[0]
-    kv_local = mid_offsets.shape[0]
-    kv_dims = (2, kv_local, HEAD_DIM)
-    kv_heads = kv_rows.reshape((tok_rows,) + kv_dims)
-    mid_kv = pick_rows(kv_heads, mid_offsets, RATE_MID, 2)
-    far_kv = pick_rows(kv_heads, far_offsets, RATE_FAR, 2)
-    mid_count = tok_rows // RATE_MID
-    far_count = tok_rows // RATE_FAR
-    far_flat = far_kv.transpose(1, 2, 0, 3).reshape(2, kv_local * far_count, HEAD_DIM)
-    return exchange(
-        queries, kv_rows, mid_kv.reshape(mid_count, -1), far_flat[0], far_flat[1],
-        mid_offsets, far_offsets,
-    )
+    )(queries, keys, values, mid_offsets, far_offsets)
 
 
 def solution(mesh):
@@ -460,5 +491,5 @@
     )
     out_specs = P(("ctx", "tensor"), None)
     return jax.shard_map(
-        on_device, mesh=mesh, in_specs=in_specs, out_specs=out_specs, check_vma=False
+        exchange, mesh=mesh, in_specs=in_specs, out_specs=out_specs, check_vma=False
     )

time: 90 us -> 81 us (0.900)
  Pallas kernels: 64 us -> 78.3 us
  starting transfers between devices: 10.4 us -> 0 us
  waiting for transfers between devices: 7.31 us -> 0 us
  local copies, waits for them, and re-layouts: 5.92 us -> 2.29 us
  other arithmetic: 2.09 us -> 0 us
    pallas_call x1, Pallas kernels: 64 us -> 78.3 us  [exchange(): pl.pallas_call(exchange_body, out_shape=jax.ShapeDtypeStruct((own, wide),...]
    all_to_all x1 -> x0, starting transfers between devices: 10.4 us -> none  [on_device(): lax.all_to_all(kv_rows, 'tensor', split_axis=1, concat_axis=0, tiled=True)]
    all_to_all x1 -> x0, waiting for transfers between devices: 7.31 us -> none  [on_device(): lax.all_to_all(kv_rows, 'tensor', split_axis=1, concat_axis=0, tiled=True)]
    reshape x2 -> x0, local copies, waits for them, and re-layouts: 1.72 us -> none  [the longest x1 1.06 us: on_device(): values.reshape(own, count, -1)]
    slice x3 -> x0, local copies, waits for them, and re-layouts: 1.2 us -> none  [the longest x2 0.61 us: on_device(): far_flat[1]]
    reduce_sum x2 -> x0, other arithmetic: 1.17 us -> none  [pick_rows(): return jnp.sum(kept, axis=1)]
    unnamed x7 -> x1, local copies, waits for them, and re-layouts: 2.88 us -> 2.29 us
  transfers between devices with their start and end apart: 1 -> 0, of which waited for: 1 -> 0; matrix products, arithmetic and copies ran while one was open for 0% -> 0% of each run, Pallas kernels for 0% -> 0%
where the time goes in v4:
time: 81 us; the launch traced here: 80.6 us
  Pallas kernels  78.3 us (97%)
  local copies, waits for them, and re-layouts  2.29 us (3%)
    pallas_call x1, Pallas kernels, exchange(): pl.pallas_call(exchange_body, out_shape=jax.ShapeDtypeStruct((own, wide),...  78.3 us
    unnamed x1, local copies, waits for them, and re-layouts  2.29 us

profile of v4, /device:TPU:1, one launch (start us, length us, event | category | flops | bytes accessed | tf_op | source)
XLA Modules:
  0.0 80.6 jit_solution(2730838307070027532)
XLA Ops:
  0.0 78.3 %exchange.1 = bf16[128,4096]{1,0:T(8,128)(2,1)} custom-call(bf16[128,4096]{1,0:T(8,128)(2,1)} %q_ref.1, bf16[128,1024]{1,0:T(8,128)(2,1)} %key_ref.1, bf16[128,1024]{1,0:T(8,128)(2,1)} %value_ref.1, s32[2]{0:T(128)} %mid_off.1, s32[2]{0:T(128)} %far_off.1), custom_call_target="tpu_custom_call" | custom-call | tf_op jit(solution)/shard_map/exchange/pallas_call | solution.py:454
  78.3 2.3 %copy.7 = bf16[128,4096]{1,0:T(8,128)(2,1)} copy(bf16[128,4096]{1,0:T(8,128)(2,1)} %exchange.1) | data formatting | bytes 2097152

commit v5 on v4

--- a/solution.py
+++ b/solution.py
@@ -218,14 +218,18 @@
     }
 
     def mid_step(step):
-        for index, block in mid_ring.landed(step - 1):
+        found = mid_ring.landed(step - 1)
+        if step <= 4:
+            mid_ring.start(step)
+        return found
+
+    def forward(found):
+        for index, block in found:
             forwards.append(
                 remote(block, block, fwd_send.at[index], fwd_recv.at[index], y_pair)
             )
-        if step <= 4:
-            mid_ring.start(step)
-
-    mid_step(2)
+
+    found = mid_step(2)
     pass_on(2)
     for step in order:
         firsts_k[step].wait_recv()
@@ -234,6 +238,7 @@
     v_ring = Ring(lambda i: fv_out.at[i], z, z_peer, v2_send, v2_recv, None, (3, 4))
     k_ring.start(1)
     v_ring.start(1)
+    forward(found)
 
     def near(chunk):
         first = chunk * CHUNK
@@ -276,7 +281,7 @@
                 max_out[head * per_group + g, first : first + CHUNK] = maxima[mine]
                 sum_out[head * per_group + g, first : first + CHUNK] = totals[mine]
 
-    mid_step(3)
+    found = mid_step(3)
     pass_on(1)
     own_q.wait()
     for copy in moves:
@@ -285,21 +290,24 @@
     k_ring.start(2)
     v_ring.landed(1)
     v_ring.start(2)
+    forward(found)
     pass_on(0)
     ahead[3].wait_recv()
     near(3)
-    mid_step(4)
+    found = mid_step(4)
     k_ring.landed(2)
     k_ring.start(3)
     v_ring.landed(2)
     v_ring.start(3)
+    forward(found)
     ahead[2].wait_recv()
     near(2)
-    mid_step(5)
+    found = mid_step(5)
     k_ring.landed(3)
     k_ring.start(4)
     v_ring.landed(3)
     v_ring.start(4)
+    forward(found)
     ahead[1].wait_recv()
     near(1)
     ahead[0].wait_recv()

time: 81 us -> 81 us (level)
  no operation moved by 1% of the time
where the time goes in v5:
time: 81 us; the launch traced here: 80.6 us
  Pallas kernels  78.3 us (97%)
  local copies, waits for them, and re-layouts  2.29 us (3%)
    pallas_call x1, Pallas kernels, exchange(): pl.pallas_call(exchange_body, out_shape=jax.ShapeDtypeStruct((own, wide),...  78.3 us
    unnamed x1, local copies, waits for them, and re-layouts  2.29 us

profile of v5, /device:TPU:1, one launch (start us, length us, event | category | flops | bytes accessed | tf_op | source)
XLA Modules:
  0.0 80.6 jit_solution(17793883930924422257)
XLA Ops:
  0.0 78.3 %exchange.1 = bf16[128,4096]{1,0:T(8,128)(2,1)} custom-call(bf16[128,4096]{1,0:T(8,128)(2,1)} %q_ref.1, bf16[128,1024]{1,0:T(8,128)(2,1)} %key_ref.1, bf16[128,1024]{1,0:T(8,128)(2,1)} %value_ref.1, s32[2]{0:T(128)} %mid_off.1, s32[2]{0:T(128)} %far_off.1), custom_call_target="tpu_custom_call" | custom-call | tf_op jit(solution)/shard_map/exchange/pallas_call | solution.py:462
  78.3 2.3 %copy.7 = bf16[128,4096]{1,0:T(8,128)(2,1)} copy(bf16[128,4096]{1,0:T(8,128)(2,1)} %exchange.1) | data formatting | bytes 2097152
